TPU v7x, 32 devices: a whole 2x2x4 slice. The times are simulated.
32 devices in a mesh: groups: 2 (over x), tm: 8 (over z, y), tile: 2 (over core).
Axes of the slice: x: 2, y: 2, z: 4, core: 2. Of those that a mesh axis runs over, the one named last changes fastest.
Arguments:
- activations: bfloat16 [64, 24, 16, 16, 128], P(('groups', 'tm'), 'tile'), parts along dimension 0, may hold values from -240 to 240
- tile_ids: int32 [48], P(('groups', 'tile')), parts along dimension 0, may hold values from 0 to 15, as said below
- tile_counts: int32 [4], P(('groups', 'tile')), parts along dimension 0, may hold values from 0 to 12, as said below
- first_gain: float32 [128], replicated, may hold values from 0.25 to 1.75
- first_shift: float32 [128], replicated, may hold values from -3 to 3
- first_conv: bfloat16 [3, 3, 3, 128, 128], replicated, may hold values from -0.109375 to 0.109375
- first_down: bfloat16 [3, 3, 3, 128, 128], replicated, may hold values from -0.109375 to 0.109375
- second_gain: float32 [128], replicated, may hold values from 0.25 to 1.75
- second_shift: float32 [128], replicated, may hold values from -3 to 3
- second_conv: bfloat16 [3, 3, 3, 128, 256], replicated, may hold values from -0.109375 to 0.109375
- second_short: bfloat16 [128, 256], replicated, may hold values from -0.5 to 0.5
- second_down: bfloat16 [3, 3, 3, 256, 256], replicated, may hold values from -0.078125 to 0.078125
Outputs:
- latents: bfloat16 [16, 16, 4, 4, 256], P(('groups', 'tm'), 'tile'), parts along dimension 0
There are 2 independent parts, one for each index of `groups`. A program takes and returns all parts, laid end to end along the dimension named above; an argument that names none is the same for every part. Nothing has to cross between parts.
Inputs may be any that keep to these rules, and one draw needn't show every extreme that they name: `tile_ids`: slot j belongs to tile device j // 12. The live slots of the two devices hold distinct tiles; tiles d * 8 to (d + 1) * 8 - 1 are owned by tile device d. Slots that are not live hold arbitrary tile numbers. The first tile_counts[d] slots of device d are live. One device holds exactly 12 live tiles, all 8 tiles of one owner among them; the other holds the remaining 4 tiles of the other owner or, for a clip of the lower resolution, none.
All inputs are finite; a program needn't handle non-finite values.
Results may differ from a plain program's by a relative error of at most 0.0066.
Values may be sent and summed in bfloat16 or wider, within the bound.
A program may use at most 64 MiB of HBM per device.

v0:
```python
import jax
import jax.numpy as jnp
from jax import lax
from jax.sharding import PartitionSpec as P

GROUPS = 32
OWN = 8


epsilon = 1e-06


def prefix(shard, axis, combine, identity):
    devices, mine = (lax.axis_size(axis), lax.axis_index(axis))
    everything = jax.tree.map(lambda part: lax.all_gather(part, axis), shard)
    start = jax.tree.map(
        lambda part, zero: jnp.broadcast_to(jnp.asarray(zero, part.dtype), part.shape),
        shard,
        identity,
    )

    def hop(k, before):
        reached = k < mine
        new = combine(before, jax.tree.map(lambda part: part[k], everything))
        return jax.tree.map(lambda a, b: jnp.where(reached, a, b), new, before)

    return lax.fori_loop(0, devices, hop, start)


def passed_along(value, axis, steps):
    count = lax.axis_size(axis)
    initial, last = (max(0, -steps), min(count, count - steps))
    return lax.ppermute(value, axis, [(source, source + steps) for source in range(initial, last)])


def group_sums(inputs):
    frames = inputs.shape[0]
    tile_count = inputs.shape[1]
    tile_side = inputs.shape[2]
    per_group = inputs.shape[4] // GROUPS
    values = inputs.astype(jnp.float32).reshape(
        frames, tile_count, tile_side * tile_side, GROUPS, per_group
    )
    return (jnp.sum(values, axis=(2, 4)), jnp.sum(values * values, axis=(2, 4)))


def normalize(inputs, total_sum, total_square, counts, norm_gain, norm_shift):
    frames = inputs.shape[0]
    tile_count = inputs.shape[1]
    tile_side = inputs.shape[2]
    per_group = inputs.shape[4] // GROUPS
    values = inputs.astype(jnp.float32).reshape(
        frames, tile_count, tile_side * tile_side, GROUPS, per_group
    )
    mean_value = total_sum / counts[:, None, None]
    spread = total_square / counts[:, None, None] - mean_value * mean_value
    inverse = lax.rsqrt(spread + epsilon)
    normed = (values - mean_value[:, :, None, :, None]) * inverse[:, :, None, :, None]
    normed = normed.reshape(inputs.shape) * norm_gain + norm_shift
    return jax.nn.silu(normed).astype(jnp.bfloat16)


def add_pairs(earlier, latter):
    return (earlier[0] + latter[0], earlier[1] + latter[1])


def earlier_sums(local_sum, local_square):
    zeros_pair = (jnp.zeros_like(local_sum), jnp.zeros_like(local_square))
    return prefix((local_sum, local_square), "tm", add_pairs, zeros_pair)


def previous_frames(inputs):
    return passed_along(inputs[-2:], "tm", 1)


def first_frames(inputs, received):
    repeated = jnp.concatenate([inputs[:1], inputs[:1]], axis=0)
    return jnp.where(lax.axis_index("tm") == 0, repeated, received)


def normed_cache(inputs, norm_gain, norm_shift):
    frames = inputs.shape[0]
    per_frame = float(inputs.shape[2] * inputs.shape[3] * (inputs.shape[4] // GROUPS))
    frame_sum, frame_square = group_sums(inputs)
    before_sum, before_square = earlier_sums(
        jnp.sum(frame_sum, axis=0), jnp.sum(frame_square, axis=0)
    )
    start_frame = lax.axis_index("tm").astype(jnp.float32) * frames
    counts = (start_frame + jnp.arange(frames, dtype=jnp.float32) + 1.0) * per_frame
    normed = normalize(
        inputs,
        before_sum + jnp.cumsum(frame_sum, axis=0),
        before_square + jnp.cumsum(frame_square, axis=0),
        counts,
        norm_gain,
        norm_shift,
    )
    received = previous_frames(normed)
    return (normed, first_frames(normed, received))


def causal_conv(inputs, cached, kernel, stride):
    padded = jnp.concatenate([cached, inputs], axis=0)
    return lax.conv_general_dilated(
        padded,
        kernel,
        (stride, stride, stride),
        ((0, 0), (1, 1), (1, 1)),
        dimension_numbers=("DNHWC", "DHWIO", "DNHWC"),
        preferred_element_type=jnp.float32,
    )


def down_cache(inputs):
    return first_frames(inputs, previous_frames(inputs))


def encode(inputs, params):
    (
        first_gain,
        first_shift,
        first_conv,
        first_down,
        second_gain,
        second_shift,
        second_conv,
        second_short,
        second_down,
    ) = params
    first_hidden, first_cached = normed_cache(inputs, first_gain, first_shift)
    first_sum = (
        inputs.astype(jnp.float32) + causal_conv(first_hidden, first_cached, first_conv, 1)
    ).astype(jnp.bfloat16)
    first_level = causal_conv(first_sum, down_cache(first_sum), first_down, 2).astype(jnp.bfloat16)
    second_hidden, second_cached = normed_cache(first_level, second_gain, second_shift)
    shortcut = jnp.einsum(
        "fkabc,cd->fkabd", first_level, second_short, preferred_element_type=jnp.float32
    )
    second_sum = (causal_conv(second_hidden, second_cached, second_conv, 1) + shortcut).astype(
        jnp.bfloat16
    )
    return causal_conv(second_sum, down_cache(second_sum), second_down, 2).astype(jnp.bfloat16)


def combine_sources(routed):
    combined = routed[:, 0:OWN]
    combined = combined + routed[:, OWN : 2 * OWN]
    return combined


def body(
    activations,
    tile_ids,
    tile_counts,
    first_gain,
    first_shift,
    first_conv,
    first_down,
    second_gain,
    second_shift,
    second_conv,
    second_short,
    second_down,
):
    params = (
        first_gain,
        first_shift,
        first_conv,
        first_down,
        second_gain,
        second_shift,
        second_conv,
        second_short,
        second_down,
    )
    owners = lax.axis_size("tile")
    tile_count = owners * OWN
    slot_live = jnp.arange(activations.shape[1]) < tile_counts[0]
    select_map = (
        (tile_ids[None, :] == jnp.arange(tile_count)[:, None]) & slot_live[None, :]
    ).astype(jnp.bfloat16)
    encoded = encode(activations, params)
    routed = jnp.einsum(
        "ks,fsabc->fkabc", select_map, encoded, preferred_element_type=jnp.float32
    ).astype(jnp.bfloat16)
    routed = lax.all_to_all(routed, "tile", split_axis=1, concat_axis=1, tiled=True)
    latents = combine_sources(routed)
    return latents


def solution(mesh):
    placed = (
        P(("groups", "tm"), "tile", None, None, None),
        P(("groups", "tile")),
        P(("groups", "tile")),
        P(),
        P(),
        P(),
        P(),
        P(),
        P(),
        P(),
        P(),
        P(),
    )
    return jax.shard_map(
        body,
        mesh=mesh,
        in_specs=placed,
        out_specs=P(("groups", "tm"), "tile", None, None, None),
        check_vma=False,
    )
```

profile of v0, /device:TPU:17, one launch (start us, length us, event | category | flops | bytes accessed | tf_op | source)
XLA Modules:
  0.0 343.3 jit_solution(2544550877958691708)
XLA Ops:
  0.0 7.2 %fusion.1 = (f32[12,128]{1,0:T(8,128)}, f32[4,12,128]{2,1,0:T(8,128)}, f32[4,12,128]{2,1,0:T(8,128)}, f32[12,128]{1,0:T(8,128)}) fusion(bf16[4,12,16,16,128]{4,3,2,1,0:T(8,128)(2,1)} %param.16), kind=kLoop, calls=%fused_computation.10 | loop fusion | flops 9421824 | bytes 3207168 | tf_op jit(solution)/shard_map/reduce_sum | solution.py:86
  11.5 22.2 %all-gather.4 = f32[8,12,32]{2,1,0:T(8,128)} all-gather(f32[1,12,32]{2,1,0:T(8,128)} %copy.31), channel_id=2, replica_groups=mesh['groups'=2,'tm'=8,'tile'=2] {'tm'}, dimensions={0}, use_global_device_ids=true | all-gather | bytes 13824 | tf_op jit(solution)/shard_map/all_gather | solution.py:15
  38.0 26.0 %all-gather.5 = f32[8,12,32]{2,1,0:T(8,128)} all-gather(f32[1,12,32]{2,1,0:T(8,128)} %copy.33), channel_id=3, replica_groups=mesh['groups'=2,'tm'=8,'tile'=2] {'tm'}, dimensions={0}, use_global_device_ids=true | all-gather | bytes 13824 | tf_op jit(solution)/shard_map/all_gather | solution.py:15
  64.1 5.8 %while.32 = (s32[]{:T(128)}, f32[12,32]{1,0:T(8,128)S(1)}, f32[12,32]{1,0:T(8,128)S(1)}, s32[]{:T(128)}, f32[8,12,32]{2,1,0:T(8,128)}, /*index=5*/f32[8,12,32]{2,1,0:T(8,128)}, s32[]{:T(128)}, s32[]{:T(128)}) while((s32[]{:T(128)}, f32[12,32]{1,0:T(8,128)S(1)}, f32[12,32]{1,0:T(8,128)S(1)}, s32[]{:T(128)}, f32[8,12,32]{2,1,0:T(8,128)}, ...), condition=%wide.region_5.6_spmd.clone, body=%wide.region_4.5_spmd.clone.sunk | while | flops 2308 | bytes 9325 | solution.py:27
  86.0 6.8 %fusion.10 = bf16[4,12,16,16,128]{4,1,3,2,0:T(8,128)(2,1)S(1)} fusion(bf16[4,12,16,16,128]{4,3,2,1,0:T(8,128)(2,1)} %param.16, f32[128]{0:T(128)} %param.20, f32[128]{0:T(128)} %param.19, f32[4,12,128]{2,1,0:T(8,128)} %copy.39, f32[4,12,128]{2,1,0:T(8,128)} %copy.36), kind=kLoop, calls=%fused_computation.19 | loop fusion | flops 15728640 | bytes 6341632 | tf_op jit(solution)/shard_map/convert_element_type | solution.py:60
  95.3 6.0 %collective-permute-start = (bf16[2,12,16,16,128]{4,3,2,1,0:T(8,128)(2,1)}, bf16[2,12,16,16,128]{4,3,2,1,0:T(8,128)(2,1)}, u32[]{:S(2)}, u32[]{:S(2)}) collective-permute-start(bf16[2,12,16,16,128]{4,3,2,1,0:T(8,128)(2,1)} %copy.40), channel_id=1, source_target_pairs={{0,2},{2,4},{4,6},{6,8},{8,10},{10,12},{12,14},{1,3},{3,5},{5,7},{... | collective-permute-start | bytes 4718600 | tf_op jit(solution)/shard_map/ppermute | solution.py:33
  102.5 19.4 %collective-permute-done = bf16[2,12,16,16,128]{4,3,2,1,0:T(8,128)(2,1)} collective-permute-done((bf16[2,12,16,16,128]{4,3,2,1,0:T(8,128)(2,1)}, bf16[2,12,16,16,128]{4,3,2,1,0:T(8,128)(2,1)}, u32[]{:S(2)}, u32[]{:S(2)}) %collective-permute-start) | collective-permute-done | bytes 1572896 | tf_op jit(solution)/shard_map/ppermute | solution.py:33
  121.8 3.1 maximum_select_fusion
  125.0 32.7 %fusion.11 = bf16[4,12,16,16,128]{4,1,3,2,0:T(8,128)(2,1)S(1)} fusion(bf16[4,12,16,16,128]{4,3,2,1,0:T(8,128)(2,1)} %param.16, bf16[3,3,3,128,128]{4,3,2,1,0:T(8,128)(2,1)} %param.21, bf16[4,12,16,16,128]{4,1,3,2,0:T(8,128)(2,1)S(1)} %copy-done.2, bf16[2,12,16,16,128]{4,1,3,2,0:T(8,128)(2,1)S(1)} %maximum_select_fusion), kind=kOutput, calls=%fused_computation.20 | convolution fusion | flops 9998696448 | bytes 11894784 | tf_op jit(solution)/shard_map/conv_general_dilated | solution.py:104
  158.1 2.0 copy.42
  160.2 4.2 %collective-permute-start.1 = (bf16[2,12,16,16,128]{4,3,2,1,0:T(8,128)(2,1)}, bf16[2,12,16,16,128]{4,3,2,1,0:T(8,128)(2,1)}, u32[]{:S(2)}, u32[]{:S(2)}) collective-permute-start(bf16[2,12,16,16,128]{4,3,2,1,0:T(8,128)(2,1)} %copy.42), channel_id=1, source_target_pairs={{0,2},{2,4},{4,6},{6,8},{8,10},{10,12},{12,14},{1,3},{3,5},{5,7},{... | collective-permute-start | bytes 4718600 | tf_op jit(solution)/shard_map/ppermute | solution.py:33
  166.8 18.2 %collective-permute-done.1 = bf16[2,12,16,16,128]{4,3,2,1,0:T(8,128)(2,1)} collective-permute-done((bf16[2,12,16,16,128]{4,3,2,1,0:T(8,128)(2,1)}, bf16[2,12,16,16,128]{4,3,2,1,0:T(8,128)(2,1)}, u32[]{:S(2)}, u32[]{:S(2)}) %collective-permute-start.1) | collective-permute-done | bytes 1572896 | tf_op jit(solution)/shard_map/ppermute | solution.py:33
  185.0 2.6 maximum_select_fusion.1
  187.6 5.3 %fusion.30 = (f32[12,128]{1,0:T(8,128)}, f32[2,12,128]{2,1,0:T(8,128)}, f32[2,12,128]{2,1,0:T(8,128)}, f32[12,128]{1,0:T(8,128)}, bf16[2,12,8,8,128]{4,1,3,2,0:T(8,128)(2,1)}) fusion(bf16[3,3,3,128,128]{4,3,2,1,0:T(8,128)(2,1)S(1)} %copy-done.9, bf16[4,12,16,16,128]{4,1,3,2,0:T(8,128)(2,1)S(1)} %copy-done.5, ...), kind=kOutput, calls=%fused_computation.42 | convolution fusion | flops 1258871808 | bytes 6033408 | tf_op jit(solution)/shard_map/conv_general_dilated | solution.py:104
  197.2 23.4 %all-gather.6 = f32[8,12,32]{2,1,0:T(8,128)} all-gather(f32[1,12,32]{2,1,0:T(8,128)} %copy.45), channel_id=4, replica_groups=mesh['groups'=2,'tm'=8,'tile'=2] {'tm'}, dimensions={0}, use_global_device_ids=true | all-gather | bytes 13824 | tf_op jit(solution)/shard_map/all_gather | solution.py:15
  224.9 26.4 %all-gather.7 = f32[8,12,32]{2,1,0:T(8,128)} all-gather(f32[1,12,32]{2,1,0:T(8,128)} %copy.47), channel_id=5, replica_groups=mesh['groups'=2,'tm'=8,'tile'=2] {'tm'}, dimensions={0}, use_global_device_ids=true | all-gather | bytes 13824 | tf_op jit(solution)/shard_map/all_gather | solution.py:15
  251.2 5.8 %while.33 = (s32[]{:T(128)}, f32[12,32]{1,0:T(8,128)S(1)}, f32[12,32]{1,0:T(8,128)S(1)}, s32[]{:T(128)}, f32[8,12,32]{2,1,0:T(8,128)}, /*index=5*/f32[8,12,32]{2,1,0:T(8,128)}, s32[]{:T(128)}, s32[]{:T(128)}) while((s32[]{:T(128)}, f32[12,32]{1,0:T(8,128)S(1)}, f32[12,32]{1,0:T(8,128)S(1)}, s32[]{:T(128)}, ...), condition=%wide.region_17.18_spmd.clone, body=%wide.region_16.17_spmd.clone.sunk | while | flops 2308 | bytes 9325 | solution.py:27
  273.1 5.8 %collective-permute-start.2 = (bf16[2,12,8,8,128]{4,1,3,2,0:T(8,128)(2,1)S(1)}, bf16[2,12,8,8,128]{4,1,3,2,0:T(8,128)(2,1)S(1)}, u32[]{:S(2)}, u32[]{:S(2)}) collective-permute-start(bf16[2,12,8,8,128]{4,1,3,2,0:T(8,128)(2,1)S(1)} %fusion.56), channel_id=1, source_target_pairs={{0,2},{2,4},{4,6},{6,8},{8,10},{10,12},{12,14},{1,3},{3,5},{5,7},{... | collective-permute-start | bytes 1179656 | tf_op jit(solution)/shard_map/ppermute | solution.py:33
  280.4 4.7 %collective-permute-done.2 = bf16[2,12,8,8,128]{4,1,3,2,0:T(8,128)(2,1)S(1)} collective-permute-done((bf16[2,12,8,8,128]{4,1,3,2,0:T(8,128)(2,1)S(1)}, bf16[2,12,8,8,128]{4,1,3,2,0:T(8,128)(2,1)S(1)}, u32[]{:S(2)}, u32[]{:S(2)}) %collective-permute-start.2) | collective-permute-done | bytes 393248 | tf_op jit(solution)/shard_map/ppermute | solution.py:33
  285.2 4.2 %add_convert_fusion = bf16[2,12,8,8,256]{4,1,3,2,0:T(8,128)(2,1)S(1)} fusion(f32[2,12,8,8,256]{4,1,3,2,0:T(8,128)S(1)} %fusion.63, bf16[3,3,3,128,256]{4,3,2,1,0:T(8,128)(2,1)S(1)} %copy-done.8, bf16[2,12,8,8,128]{4,1,3,2,0:T(8,128)(2,1)S(1)} %fusion.56, bf16[2,12,8,8,128]{4,1,3,2,0:T(8,128)(2,1)S(1)} %maximum_select_fusion.3), kind=kOutput, calls=%fused_computation.35 | convolution fusion | flops 2286157824 | bytes 4915200 | tf_op jit(solution)/shard_map/conv_general_dilated | solution.py:104
  289.7 3.8 %collective-permute-start.3 = (bf16[2,12,8,8,256]{4,3,2,1,0:T(8,128)(2,1)S(1)}, bf16[2,12,8,8,256]{4,3,2,1,0:T(8,128)(2,1)S(1)}, u32[]{:S(2)}, u32[]{:S(2)}) collective-permute-start(bf16[2,12,8,8,256]{4,3,2,1,0:T(8,128)(2,1)S(1)} %copy.56), channel_id=1, source_target_pairs={{0,2},{2,4},{4,6},{6,8},{8,10},{10,12},{12,14},{1,3},{3,5},{5,7},{... | collective-permute-start | bytes 2359304 | tf_op jit(solution)/shard_map/ppermute | solution.py:33
  294.2 9.1 %collective-permute-done.3 = bf16[2,12,8,8,256]{4,3,2,1,0:T(8,128)(2,1)S(1)} collective-permute-done((bf16[2,12,8,8,256]{4,3,2,1,0:T(8,128)(2,1)S(1)}, bf16[2,12,8,8,256]{4,3,2,1,0:T(8,128)(2,1)S(1)}, u32[]{:S(2)}, u32[]{:S(2)}) %collective-permute-start.3) | collective-permute-done | bytes 786464 | tf_op jit(solution)/shard_map/ppermute | solution.py:33
  304.9 3.3 fusion.37
  309.2 33.5 %all_to_all.5 = bf16[1,16,4,4,256]{4,3,2,0,1:T(4,128)(2,1)S(1)} all-to-all(bf16[1,16,4,4,256]{4,3,2,0,1:T(4,128)(2,1)S(1)} %copy.58), channel_id=1, replica_groups=mesh['groups'=2,'tm'=8,'tile'=2] {'tile'}, dimensions={1} | all-to-all | bytes 262144 | tf_op jit(solution)/shard_map/all_to_all | solution.py:186
  (95 shorter events, 72.5 us)
Async XLA Ops:
  0.0 304.9 %copy-start = (bf16[3,3,3,256,256]{4,3,2,1,0:T(8,128)(2,1)S(1)}, bf16[3,3,3,256,256]{4,3,2,1,0:T(8,128)(2,1)}, u32[]{:S(2)}) copy-start(bf16[3,3,3,256,256]{4,3,2,1,0:T(8,128)(2,1)} %param.27) | copy-start | bytes 10616836
  78.8 0.6 copy-start.6
  92.8 8.5 %copy-start.1 = (bf16[4,12,16,16,128]{4,1,3,2,0:T(8,128)(2,1)}, bf16[4,12,16,16,128]{4,1,3,2,0:T(8,128)(2,1)S(1)}, u32[]{:S(2)}) copy-start(bf16[4,12,16,16,128]{4,1,3,2,0:T(8,128)(2,1)S(1)} %fusion.10) | copy-start | bytes 9437188
  95.3 26.5 %collective-permute-start = (bf16[2,12,16,16,128]{4,3,2,1,0:T(8,128)(2,1)}, bf16[2,12,16,16,128]{4,3,2,1,0:T(8,128)(2,1)}, u32[]{:S(2)}, u32[]{:S(2)}) collective-permute-start(bf16[2,12,16,16,128]{4,3,2,1,0:T(8,128)(2,1)} %copy.40), channel_id=1, source_target_pairs={{0,2},{2,4},{4,6},{6,8},{8,10},{10,12},{12,14},{1,3},{3,5},{5,7},{... | collective-permute-start | bytes 4718600 | tf_op jit(solution)/shard_map/ppermute | solution.py:33
  102.5 22.5 %copy-start.2 = (bf16[4,12,16,16,128]{4,1,3,2,0:T(8,128)(2,1)S(1)}, bf16[4,12,16,16,128]{4,1,3,2,0:T(8,128)(2,1)}, u32[]{:S(2)}) copy-start(bf16[4,12,16,16,128]{4,1,3,2,0:T(8,128)(2,1)} %copy-done.1) | copy-start | bytes 9437188
  157.7 2.5 copy-start.4
  160.2 24.8 %collective-permute-start.1 = (bf16[2,12,16,16,128]{4,3,2,1,0:T(8,128)(2,1)}, bf16[2,12,16,16,128]{4,3,2,1,0:T(8,128)(2,1)}, u32[]{:S(2)}, u32[]{:S(2)}) collective-permute-start(bf16[2,12,16,16,128]{4,3,2,1,0:T(8,128)(2,1)} %copy.42), channel_id=1, source_target_pairs={{0,2},{2,4},{4,6},{6,8},{8,10},{10,12},{12,14},{1,3},{3,5},{5,7},{... | collective-permute-start | bytes 4718600 | tf_op jit(solution)/shard_map/ppermute | solution.py:33
  164.4 23.1 %copy-start.5 = (bf16[4,12,16,16,128]{4,1,3,2,0:T(8,128)(2,1)S(1)}, bf16[4,12,16,16,128]{4,1,3,2,0:T(8,128)(2,1)}, u32[]{:S(2)}) copy-start(bf16[4,12,16,16,128]{4,1,3,2,0:T(8,128)(2,1)} %copy-done.4) | copy-start | bytes 9437188
  164.4 23.1 %copy-start.9 = (bf16[3,3,3,128,128]{4,3,2,1,0:T(8,128)(2,1)S(1)}, bf16[3,3,3,128,128]{4,3,2,1,0:T(8,128)(2,1)}, u32[]{:S(2)}) copy-start(bf16[3,3,3,128,128]{4,3,2,1,0:T(8,128)(2,1)} %param.22) | copy-start | bytes 2654212
  265.4 0.6 copy-start.7
  271.5 13.7 %copy-start.8 = (bf16[3,3,3,128,256]{4,3,2,1,0:T(8,128)(2,1)S(1)}, bf16[3,3,3,128,256]{4,3,2,1,0:T(8,128)(2,1)}, u32[]{:S(2)}) copy-start(bf16[3,3,3,128,256]{4,3,2,1,0:T(8,128)(2,1)} %param.25) | copy-start | bytes 5308420
  273.1 12.0 %collective-permute-start.2 = (bf16[2,12,8,8,128]{4,1,3,2,0:T(8,128)(2,1)S(1)}, bf16[2,12,8,8,128]{4,1,3,2,0:T(8,128)(2,1)S(1)}, u32[]{:S(2)}, u32[]{:S(2)}) collective-permute-start(bf16[2,12,8,8,128]{4,1,3,2,0:T(8,128)(2,1)S(1)} %fusion.56), channel_id=1, source_target_pairs={{0,2},{2,4},{4,6},{6,8},{8,10},{10,12},{12,14},{1,3},{3,5},{5,7},{... | collective-permute-start | bytes 1179656 | tf_op jit(solution)/shard_map/ppermute | solution.py:33
  289.4 4.8 %copy-start.3 = (bf16[2,12,8,8,256]{4,1,3,2,0:T(8,128)(2,1)}, bf16[2,12,8,8,256]{4,1,3,2,0:T(8,128)(2,1)S(1)}, u32[]{:S(2)}) copy-start(bf16[2,12,8,8,256]{4,1,3,2,0:T(8,128)(2,1)S(1)} %add_convert_fusion) | copy-start | bytes 2359300
  289.4 15.5 %copy-start.10 = (s32[12]{0:T(128)S(1)}, s32[12]{0:T(128)}, u32[]{:S(2)}) copy-start(s32[12]{0:T(128)} %param.17) | copy-start | bytes 148
  289.7 13.6 %collective-permute-start.3 = (bf16[2,12,8,8,256]{4,3,2,1,0:T(8,128)(2,1)S(1)}, bf16[2,12,8,8,256]{4,3,2,1,0:T(8,128)(2,1)S(1)}, u32[]{:S(2)}, u32[]{:S(2)}) collective-permute-start(bf16[2,12,8,8,256]{4,3,2,1,0:T(8,128)(2,1)S(1)} %copy.56), channel_id=1, source_target_pairs={{0,2},{2,4},{4,6},{6,8},{8,10},{10,12},{12,14},{1,3},{3,5},{5,7},{... | collective-permute-start | bytes 2359304 | tf_op jit(solution)/shard_map/ppermute | solution.py:33
where the time goes:
time: 349 us; the launch traced here: 343 us
  blocking collectives  132 us (38%)
  other arithmetic  51.9 us (15%)
  waiting for transfers between devices  51.3 us (15%)
  matrix products  47 us (13%)
  local copies, waits for them, and re-layouts  40.9 us (12%)
  starting transfers between devices  19.8 us (6%)
    all_gather x4, blocking collectives, prefix(): everything = jax.tree.map(lambda part: lax.all_gather(part, axis), shard)  98 us
    ppermute x4, waiting for transfers between devices, passed_along(): lax.ppermute(value, axis, [(source, source + steps) for source in range(i...  51.3 us
    conv_general_dilated x3, matrix products, causal_conv(): lax.conv_general_dilated(padded, kernel, (stride, stride, stride), ((0, 0...  42.2 us
    all_to_all x1, blocking collectives, body(): lax.all_to_all(routed, 'tile', split_axis=1, concat_axis=1, tiled=True)  33.5 us
    ppermute x4, starting transfers between devices, passed_along(): lax.ppermute(value, axis, [(source, source + steps) for source in range(i...  19.8 us
    select_n x16, other arithmetic, hop(): return jax.tree.map(lambda a, b: jnp.where(reached, a, b), new, before)  11.5 us
    reduce_sum x3, other arithmetic, normed_cache(): jnp.sum(frame_square, axis=0)  10.1 us
    convert_element_type x2, other arithmetic, normalize(): return jax.nn.silu(normed).astype(jnp.bfloat16)  8.39 us
  transfers between devices with their start and end apart: 4, of which 4 were waited for; matrix products, arithmetic and copies ran while one was open for 1% of the time, Pallas kernels for 0%

commit v1 on v0

v1 whole, which is shorter than its diff:
```python
import functools

import jax
import jax.numpy as jnp
import numpy as np
from jax import lax
from jax.experimental import pallas as pl
from jax.experimental.pallas import tpu as pltpu
from jax.sharding import PartitionSpec as P

GROUPS = 32
OWN = 8
MOVED = 4
EPS = 1e-06
F32 = jnp.float32
BF16 = jnp.bfloat16
MESH = pl.DeviceIdType.MESH
VMEM = pl.BlockSpec(memory_space=pltpu.VMEM)
LIMIT = 56 << 20


def full(shape):
    return pl.BlockSpec(shape, lambda j, *_: (0,) * len(shape))


def prep_kernel(flag, own_ref, recv_ref, xa_ref, xb_ref, sums_ref):
    j = pl.program_id(0)
    keep = jnp.logical_or(j < OWN - MOVED, flag[0] == 1)

    def put(ref):
        for f in range(4):
            v = ref[f, 0]
            out = xa_ref if f < 2 else xb_ref
            out[f % 2, 0] = v
            w = v.astype(F32).reshape(256, 128)
            sums_ref[0, f, 0:1] = jnp.sum(w, axis=0, keepdims=True)
            sums_ref[0, f, 1:2] = jnp.sum(w * w, axis=0, keepdims=True)

    @pl.when(keep)
    def _():
        put(own_ref)

    @pl.when(jnp.logical_not(keep))
    def _():
        put(recv_ref)


def prep(acts, recv, flag):
    cells = acts.shape[2:]
    block = (4, 1) + cells
    pair = (2, 1) + cells
    return pl.pallas_call(
        prep_kernel,
        out_shape=(
            jax.ShapeDtypeStruct((2, OWN) + cells, BF16),
            jax.ShapeDtypeStruct((2, OWN) + cells, BF16),
            jax.ShapeDtypeStruct((OWN, 4, 2, 128), F32),
        ),
        grid_spec=pltpu.PrefetchScalarGridSpec(
            num_scalar_prefetch=1,
            grid=(OWN,),
            in_specs=[
                pl.BlockSpec(block, lambda j, f: (0, j, 0, 0, 0)),
                pl.BlockSpec(block, lambda j, f: (0, jnp.maximum(j - MOVED, 0), 0, 0, 0)),
            ],
            out_specs=[
                pl.BlockSpec(pair, lambda j, f: (0, j, 0, 0, 0)),
                pl.BlockSpec(pair, lambda j, f: (0, j, 0, 0, 0)),
                pl.BlockSpec((1, 4, 2, 128), lambda j, f: (j, 0, 0, 0)),
            ],
        ),
        name="prep",
        compiler_params=pltpu.CompilerParams(vmem_limit_bytes=LIMIT),
    )(flag, acts, recv)


def stats_kernel(n, frames, per_frame, s_ref, g_ref, out_ref, mine, got, send, recv):
    me = lax.axis_index("tm")
    barrier = pltpu.get_barrier_semaphore()
    for k in range(1, n):
        pl.semaphore_signal(barrier, inc=1, device_id={"tm": lax.rem(me + k, n)}, device_id_type=MESH)
    partial = s_ref[0]
    for f in range(1, frames - 1):
        partial = partial + s_ref[f]
    mine[1] = partial
    mine[0] = partial + s_ref[frames - 1]
    pl.semaphore_wait(barrier, n - 1)
    copies = []
    for k in range(1, n):
        src, dst = (mine, got.at[k]) if k == 1 else (mine.at[0], got.at[k, 0])
        c = pltpu.make_async_remote_copy(
            src_ref=src,
            dst_ref=dst,
            send_sem=send.at[k],
            recv_sem=recv.at[k],
            device_id={"tm": lax.rem(me + k, n)},
            device_id_type=MESH,
        )
        c.start()
        copies.append(c)
    rest = jnp.zeros_like(partial)
    for k in range(n - 1, 1, -1):
        copies[k - 1].wait()
        rest = rest + jnp.where(k <= me, got[k, 0], 0.0)
    copies[0].wait()
    before = rest + jnp.where(me >= 1, got[1, 0], 0.0)
    before2 = rest + jnp.where(me >= 1, got[1, 1], 0.0)
    rows = [before2, before]
    run = before
    for f in range(frames):
        run = run + s_ref[f]
        rows.append(run)
    ri = lax.broadcasted_iota(jnp.int32, (128, 128), 0) // (128 // GROUPS)
    ci = lax.broadcasted_iota(jnp.int32, (128, 128), 1) // (128 // GROUPS)
    same = jnp.where(ri == ci, 1.0, 0.0).astype(F32)
    start = (me * frames).astype(F32)
    made = []
    for i, r in enumerate(rows):
        count = jnp.maximum(start + float(i - 1), 1.0) * per_frame
        inv_count = jnp.full((1, 128), 1.0, F32) / (jnp.zeros((1, 128), F32) + count)
        g = jnp.dot(r, same, precision=lax.Precision.HIGHEST, preferred_element_type=F32)
        m = g[0:OWN] * inv_count
        var = g[OWN : 2 * OWN] * inv_count - m * m
        made.append((m, lax.rsqrt(var + EPS) * g_ref[...]))
    for i in range(frames + 2):
        m, s = made[i]
        if i < 2:
            m = jnp.where(me == 0, made[2][0], m)
            s = jnp.where(me == 0, made[2][1], s)
        out_ref[i, 0] = m
        out_ref[i, 1] = s


def stats(sums, gain, n, per_frame, cid):
    frames = sums.shape[0]
    return pl.pallas_call(
        functools.partial(stats_kernel, n, frames, per_frame),
        out_shape=jax.ShapeDtypeStruct((frames + 2, 2, OWN, 128), F32),
        in_specs=[VMEM, VMEM],
        out_specs=VMEM,
        scratch_shapes=[
            pltpu.VMEM((2, 2 * OWN, 128), F32),
            pltpu.VMEM((n, 2, 2 * OWN, 128), F32),
            pltpu.SemaphoreType.DMA((n,)),
            pltpu.SemaphoreType.DMA((n,)),
        ],
        name="stats" + str(cid),
        compiler_params=pltpu.CompilerParams(collective_id=cid, has_side_effects=True),
    )(sums, gain.reshape(1, 128))


def silu(u):
    return (0.5 * u) * (1.0 + jnp.tanh(0.5 * u))


def shifted(v, side):
    rows = v.shape[0]
    col = lax.broadcasted_iota(jnp.int32, v.shape, 0) % side
    left = jnp.where(col == 0, 0.0, pltpu.roll(v, 1, axis=0))
    right = jnp.where(col == side - 1, 0.0, pltpu.roll(v, rows - 1, axis=0))
    return left, right


def first_kernel(base, second, flag, *refs):
    xa_ref, xb_ref, p_ref, shift_ref, conv_ref, down_ref = refs[:6]
    if second:
        prev_ref, got_ref, level_ref, sums_ref = refs[6:10]
    else:
        own_ref, next_ref = refs[6:8]
    buf, w2, wd, sf, lhs = refs[-5:]
    j = pl.program_id(0)

    @pl.when(j == 0)
    def _():
        zero = jnp.zeros((128, 128), BF16)
        for q in range(4):
            for b in range(3):
                for c in range(3):
                    for e in range(2):
                        a = q - e
                        k = (q % 2) * 384 + c * 128
                        w2[(q // 2) * 3 + b, k : k + 128, e * 128 : e * 128 + 128] = (
                            conv_ref[a, b, c] if 0 <= a < 3 else zero
                        )
        for b in range(3):
            for c in range(3):
                wd[b, c * 128 : c * 128 + 128, 0:128] = down_ref[2, b, c]
                wd[b, 384 + c * 128 : 512 + c * 128, 0:128] = zero
                wd[b, c * 128 : c * 128 + 128, 128:256] = down_ref[0, b, c]
                wd[b, 384 + c * 128 : 512 + c * 128, 128:256] = down_ref[1, b, c]
        edge = jnp.zeros((16, 768), BF16)
        for p in range(2):
            buf[p, 0:16] = edge
            buf[p, 272:288] = edge

    for q in range(4):
        x = (xa_ref if q < 2 else xb_ref)[q % 2, 0].astype(F32).reshape(256, 128)
        if second and q < 2:
            x = jnp.where(flag[0] == 1, xb_ref[0, 0].astype(F32).reshape(256, 128), x)
        mean = p_ref[base + q, 0, pl.ds(j, 1), :]
        scale = p_ref[base + q, 1, pl.ds(j, 1), :]
        h = silu((x - mean) * scale + shift_ref[...])
        left, right = shifted(h, 16)
        k = (q % 2) * 384
        buf[q // 2, 16:272, k : k + 128] = left.astype(BF16)
        buf[q // 2, 16:272, k + 128 : k + 256] = h.astype(BF16)
        buf[q // 2, 16:272, k + 256 : k + 384] = right.astype(BF16)
    acc = jnp.zeros((256, 256), F32)
    for p in range(2):
        for b in range(3):
            acc = acc + jnp.dot(buf[p, b * 16 : b * 16 + 256, :], w2[p * 3 + b], preferred_element_type=F32)
    for e in range(2):
        x = xb_ref[e, 0].astype(F32).reshape(256, 128)
        sf[e] = (x + acc[:, e * 128 : e * 128 + 128]).astype(BF16).astype(F32)
    row = pl.multiple_of(j * 64, 64)
    col = lax.broadcasted_iota(jnp.int32, (128, 128), 0) % 8
    for e in range(2):
        even = sf[e, pl.ds(0, 128, stride=2), :]
        odd = sf[e, pl.ds(1, 128, stride=2), :]
        prev = jnp.where(col == 0, 0.0, pltpu.roll(odd, 1, axis=0))
        for c, v in enumerate((prev, even, odd)):
            v = v.reshape(8, 2, 8, 128)
            top, low = v[:, 0], v[:, 1]
            up = jnp.concatenate([jnp.zeros((1, 8, 128), F32), low[:7]], axis=0)
            k = e * 384 + c * 128
            for b, u in enumerate((up, top, low)):
                lhs[b, pl.ds(row, 64), k : k + 128] = u.reshape(64, 128).astype(BF16)

    @pl.when(j == OWN - 1)
    def _():
        out = jnp.zeros((512, 256), F32)
        for b in range(3):
            out = out + jnp.dot(lhs[b], wd[b], preferred_element_type=F32)
        if not second:
            own_ref[...] = out[:, 0:128]
            next_ref[...] = out[:, 128:256]
        else:
            sf0 = got_ref[...] + out[:, 0:128]
            got_ref[...] = sf0
            last = (prev_ref[...] + out[:, 128:256]).astype(BF16)
            level_ref[1] = last

            @pl.when(flag[0] == 1)
            def _():
                extra = got_ref[...]
                for b in range(3):
                    twice = jnp.concatenate([lhs[b, :, 0:384], lhs[b, :, 0:384]], axis=1)
                    extra = extra + jnp.dot(twice, wd[b, :, 128:256], preferred_element_type=F32)
                got_ref[...] = extra

            level_ref[0] = got_ref[...].astype(BF16)
            for f in range(2):
                v = level_ref[f].astype(F32).reshape(OWN, 64, 128)
                sums_ref[f, 0:OWN] = jnp.sum(v, axis=1)
                sums_ref[f, OWN : 2 * OWN] = jnp.sum(v * v, axis=1)


def first_pair(xa, xb, params, shift, conv, down, flag, prev=None, got=None):
    second = prev is not None
    cells = xa.shape[2:]
    pair = pl.BlockSpec((2, 1) + cells, lambda j, f: (0, j, 0, 0, 0))
    rows = OWN * 64
    in_specs = [pair, pair, full(params.shape), full((1, 128)), full(conv.shape), full(down.shape)]
    args = [xa, xb, params, shift.reshape(1, 128), conv, down]
    if second:
        in_specs += [full((rows, 128))] * 2
        args += [prev, got]
        outs = (jax.ShapeDtypeStruct((2, rows, 128), BF16), jax.ShapeDtypeStruct((2, 2 * OWN, 128), F32))
    else:
        outs = (jax.ShapeDtypeStruct((rows, 128), F32),) * 2
    return pl.pallas_call(
        functools.partial(first_kernel, 0 if second else 2, second),
        out_shape=outs,
        grid_spec=pltpu.PrefetchScalarGridSpec(
            num_scalar_prefetch=1,
            grid=(OWN,),
            in_specs=in_specs,
            out_specs=[full(o.shape) for o in outs],
            scratch_shapes=[
                pltpu.VMEM((2, 288, 768), BF16),
                pltpu.VMEM((6, 768, 256), BF16),
                pltpu.VMEM((3, 768, 256), BF16),
                pltpu.VMEM((2, 256, 128), F32),
                pltpu.VMEM((3, rows, 768), BF16),
            ],
        ),
        name="firstb" if second else "firsta",
        cost_estimate=pl.CostEstimate(flops=8 * 10**9, bytes_accessed=6 * 10**6, transcendentals=10**6),
        compiler_params=pltpu.CompilerParams(vmem_limit_bytes=LIMIT),
    )(flag, *args)


def second_kernel(flag, halo_ref, lev_ref, p_ref, shift_ref, conv_ref, short_ref, down_ref, pick_ref, own_ref, next_ref, lhs):
    for t in range(OWN):
        for q in range(4):
            lo, hi = t * 64, t * 64 + 64
            if q < 2:
                x = jnp.where(flag[0] == 1, lev_ref[0, lo:hi].astype(F32), halo_ref[q, lo:hi].astype(F32))
            else:
                x = lev_ref[q - 2, lo:hi].astype(F32)
            h = silu((x - p_ref[q, 0, t : t + 1, :]) * p_ref[q, 1, t : t + 1, :] + shift_ref[...])
            left, right = shifted(h, 8)
            zero = jnp.zeros((8, 128), F32)
            for c, v in enumerate((left, h, right)):
                for b, u in enumerate(
                    (jnp.concatenate([zero, v[:56]], axis=0), v, jnp.concatenate([v[8:], zero], axis=0))
                ):
                    k = (b * 3 + c) * 128
                    lhs[q, lo:hi, k : k + 128] = u.astype(BF16)
    level2 = []
    for f in range(2):
        acc = jnp.dot(lev_ref[f], short_ref[...], preferred_element_type=F32)
        for a in range(3):
            acc = acc + jnp.dot(lhs[f + a], conv_ref[a], preferred_element_type=F32)
        level2.append(acc.astype(BF16))
    own = jnp.zeros((128, 256), F32)
    nxt = jnp.zeros((128, 256), F32)
    first = []
    for i in range(9):
        pick = pick_ref[i * 128 : i * 128 + 128]
        s0 = jnp.dot(pick, level2[0], preferred_element_type=F32).astype(BF16)
        s1 = jnp.dot(pick, level2[1], preferred_element_type=F32).astype(BF16)
        own = own + jnp.dot(s0, down_ref[18 + i], preferred_element_type=F32)
        nxt = nxt + jnp.dot(s0, down_ref[i], preferred_element_type=F32)
        nxt = nxt + jnp.dot(s1, down_ref[9 + i], preferred_element_type=F32)
        lhs[0, i * 0 : 128, i * 128 : i * 128 + 128] = s0[:, 0:128]
        lhs[1, i * 0 : 128, i * 128 : i * 128 + 128] = s0[:, 128:256]
    own_ref[...] = own
    next_ref[...] = nxt

    @pl.when(flag[0] == 1)
    def _():
        extra = own_ref[...]
        for i in range(9):
            s0 = jnp.concatenate(
                [lhs[0, 0:128, i * 128 : i * 128 + 128], lhs[1, 0:128, i * 128 : i * 128 + 128]], axis=1
            )
            extra = extra + jnp.dot(s0, down_ref[i], preferred_element_type=F32)
            extra = extra + jnp.dot(s0, down_ref[9 + i], preferred_element_type=F32)
        own_ref[...] = extra


def pick_matrix():
    m = np.zeros((9, OWN, 4, 4, OWN, 8, 8), np.float32)
    for b in range(3):
        for c in range(3):
            for y in range(4):
                for x in range(4):
                    h, w = 2 * y + b - 1, 2 * x + c - 1
                    if 0 <= h < 8 and 0 <= w < 8:
                        for t in range(OWN):
                            m[b * 3 + c, t, y, x, t, h, w] = 1.0
    return m.reshape(9 * OWN * 16, OWN * 64)


def second_block(halo, level, params, shift, conv, short, down, flag):
    out = jax.ShapeDtypeStruct((OWN * 16, 256), F32)
    return pl.pallas_call(
        second_kernel,
        out_shape=(out, out),
        in_specs=[pl.BlockSpec(memory_space=pltpu.SMEM)] + [VMEM] * 8,
        out_specs=[VMEM, VMEM],
        scratch_shapes=[pltpu.VMEM((4, OWN * 64, 1152), BF16)],
        name="secondk",
        compiler_params=pltpu.CompilerParams(vmem_limit_bytes=LIMIT),
    )(
        flag,
        halo,
        level,
        params,
        shift.reshape(1, 128),
        conv.reshape(3, 1152, 256),
        short,
        down.reshape(27, 256, 256),
        jnp.asarray(pick_matrix(), BF16),
    )


def passed(value, axis):
    count = lax.axis_size(axis)
    return lax.ppermute(value, axis, [(i, i + 1) for i in range(count - 1)])


def swapped(value):
    return lax.ppermute(value, "tile", [(0, 1), (1, 0)])


def body(
    activations,
    tile_ids,
    tile_counts,
    first_gain,
    first_shift,
    first_conv,
    first_down,
    second_gain,
    second_shift,
    second_conv,
    second_short,
    second_down,
):
    n = lax.axis_size("tm")
    me = lax.axis_index("tile")
    start = (lax.axis_index("tm") == 0).astype(jnp.int32).reshape(1)
    cap = activations.shape[1]
    recv = swapped(activations[:, OWN:cap])
    info = jnp.concatenate([tile_ids, tile_counts])
    other = swapped(info)
    heavy = (tile_counts[0] == cap).astype(jnp.int32).reshape(1)

    def encoded_ids(a, b):
        slots = jnp.arange(cap)
        ids_a = jnp.where(slots < a[cap], a[:cap], -1)
        ids_b = jnp.where(slots < b[cap], b[:cap], -1)
        kept = jnp.where(a[cap] == cap, ids_a[OWN - MOVED : OWN], ids_b[OWN:])
        return jnp.concatenate([ids_a[: OWN - MOVED], kept])

    ids = jnp.concatenate([encoded_ids(info, other), encoded_ids(other, info)])

    xa, xb, sums = prep(activations, recv, heavy)
    halo = passed(xb, "tm")
    sums = sums.transpose(1, 2, 0, 3).reshape(4, 2 * OWN, 128)
    side = activations.shape[2]
    params = stats(sums, first_gain, n, float(side * side * (128 // GROUPS)), 0)
    own1, next1 = first_pair(xa, xb, params, first_shift, first_conv, first_down, start)
    got1 = passed(next1, "tm")
    level, sums2 = first_pair(halo, xa, params, first_shift, first_conv, first_down, start, own1, got1)
    halo2 = passed(level, "tm")
    params2 = stats(sums2, second_gain, n, float(side * side // 4 * (128 // GROUPS)), 1)
    own2, next2 = second_block(halo2, level, params2, second_shift, second_conv, second_short, second_down, start)
    enc = (own2 + passed(next2, "tm")).astype(BF16).reshape(OWN, 16 * 256)
    both = jnp.concatenate([enc, swapped(enc)], axis=0)
    select = (ids[None, :] == (me * OWN + jnp.arange(OWN))[:, None]).astype(BF16)
    latents = jnp.dot(select, both, preferred_element_type=F32).astype(BF16)
    return latents.reshape(1, OWN, 4, 4, 256)


def solution(mesh):
    placed = (
        P(("groups", "tm"), "tile", None, None, None),
        P(("groups", "tile")),
        P(("groups", "tile")),
    ) + (P(),) * 9
    return jax.shard_map(
        body,
        mesh=mesh,
        in_specs=placed,
        out_specs=P(("groups", "tm"), "tile", None, None, None),
        check_vma=False,
    )
```

time: 349 us -> 112 us (0.32); the launches traced: 343 us -> 111 us
  blocking collectives: 132 us -> 0 us
  Pallas kernels: 0 us -> 72.5 us
  other arithmetic: 51.9 us -> 1.8 us
  matrix products: 47 us -> 0.2 us
  waiting for transfers between devices: 51.3 us -> 10.8 us
  local copies, waits for them, and re-layouts: 40.9 us -> 6.87 us
    all_gather x4 -> x0, blocking collectives: 98 us -> none  [prefix(): everything = jax.tree.map(lambda part: lax.all_gather(part, axis), shard)]
    pallas_call x0 -> x6, Pallas kernels: none -> 72.5 us  [the longest x2 33.3 us: stats(): pl.pallas_call(functools.partial(stats_kernel, n, frames, per_frame), out...]
    conv_general_dilated x3 -> x0, matrix products: 42.2 us -> none  [causal_conv(): lax.conv_general_dilated(padded, kernel, (stride, stride, stride), ((0, 0...]
    ppermute x4 -> x7, waiting for transfers between devices: 51.3 us -> 10.8 us  [the longest x4 8.39 us: passed(): return lax.ppermute(value, axis, [(i, i + 1) for i in range(count - 1)])]
    all_to_all x1 -> x0, blocking collectives: 33.5 us -> none  [body(): lax.all_to_all(routed, 'tile', split_axis=1, concat_axis=1, tiled=True)]
    reduce_sum x9 -> x0, other arithmetic: 19.7 us -> none  [the longest x3 10.1 us: normed_cache(): jnp.sum(frame_square, axis=0)]
    select_n x20 -> x3, other arithmetic: 18.9 us -> 0.71 us  [the longest x1 0.64 us: encoded_ids(): ids_b = jnp.where(slots < b[cap], b[:cap], -1)]
    reduce_sum x8 -> x0, local copies, waits for them, and re-layouts: 11.9 us -> none  [the longest x4 6.14 us: group_sums(): return (jnp.sum(values, axis=(2, 4)), jnp.sum(values * values, axis=(2, 4)))]
  transfers between devices with their start and end apart: 4 -> 7, of which waited for: 4 -> 4; matrix products, arithmetic and copies ran while one was open for 1% -> 3% of each run, Pallas kernels for 0% -> 52%
where the time goes in v1:
time: 112 us; the launch traced here: 111 us
  Pallas kernels  72.5 us (65%)
  starting transfers between devices  17.8 us (16%)
  waiting for transfers between devices  10.8 us (10%)
  local copies, waits for them, and re-layouts  6.87 us (6%)
  other arithmetic  1.8 us (2%)
  between operations  1.43 us (1%)
    pallas_call x2, Pallas kernels, stats(): pl.pallas_call(functools.partial(stats_kernel, n, frames, per_frame), out...  33.3 us
    pallas_call x2, Pallas kernels, first_pair(): pl.pallas_call(functools.partial(first_kernel, 0 if second else 2, second...  24.6 us
    ppermute x4, starting transfers between devices, passed(): return lax.ppermute(value, axis, [(i, i + 1) for i in range(count - 1)])  10 us
    ppermute x4, waiting for transfers between devices, passed(): return lax.ppermute(value, axis, [(i, i + 1) for i in range(count - 1)])  8.39 us
    pallas_call x1, Pallas kernels, second_block(): pl.pallas_call(second_kernel, out_shape=(out, out), in_specs=[pl.BlockSpe...  8.37 us
    ppermute x3, starting transfers between devices, swapped(): return lax.ppermute(value, 'tile', [(0, 1), (1, 0)])  7.77 us
    pallas_call x1, Pallas kernels, prep(): pl.pallas_call(prep_kernel, out_shape=(jax.ShapeDtypeStruct((2, OWN) + ce...  6.25 us
    unnamed x10, local copies, waits for them, and re-layouts  2.75 us
  transfers between devices with their start and end apart: 7, of which 4 were waited for; matrix products, arithmetic and copies ran while one was open for 3% of the time, Pallas kernels for 52%

profile of v1, /device:TPU:17, one launch (start us, length us, event | category | flops | bytes accessed | tf_op | source)
XLA Modules:
  0.0 111.5 jit_solution(3027281423060315424)
XLA Ops:
  0.0 1.4 %slice.38 = bf16[4,4,16,16,128]{4,3,2,1,0:T(8,128)(2,1)S(1)} slice(bf16[4,12,16,16,128]{4,3,2,1,0:T(8,128)(2,1)} %own_ref.1), slice={[0:4], [8:12], [0:16], [0:16], [0:128]} | slice | bytes 2097152 | tf_op jit(solution)/shard_map/slice | solution.py:406
  1.4 0.7 collective-permute-start.1
  2.8 1.6 %collective-permute-done.1.recv_ref = bf16[4,4,16,16,128]{4,3,2,1,0:T(8,128)(2,1)S(1)} collective-permute-done((bf16[4,4,16,16,128]{4,3,2,1,0:T(8,128)(2,1)S(1)}, bf16[4,4,16,16,128]{4,3,2,1,0:T(8,128)(2,1)S(1)}, u32[]{:S(2)}, u32[]{:S(2)}) %collective-permute-start.1) | collective-permute-done | bytes 1048608 | tf_op jit(solution)/shard_map/ppermute | solution.py:385
  4.4 1.0 copy-done
  5.4 6.3 %prep.1 = (bf16[2,8,16,16,128]{4,3,2,1,0:T(8,128)(2,1)}, bf16[2,8,16,16,128]{4,3,2,1,0:T(8,128)(2,1)}, f32[8,4,2,128]{3,2,1,0:T(2,128)}) custom-call(s32[1]{0:T(128)} %bitcast.3.flag, bf16[4,12,16,16,128]{4,3,2,1,0:T(8,128)(2,1)} %own_ref.1, bf16[4,4,16,16,128]{4,3,2,1,0:T(8,128)(2,1)} %copy-done), custom_call_target="tpu_custom_call" | custom-call | tf_op jit(solution)/shard_map/prep/pallas_call | solution.py:52
  11.7 3.1 %collective-permute-start.2 = (bf16[2,8,16,16,128]{4,3,2,1,0:T(8,128)(2,1)}, bf16[2,8,16,16,128]{4,3,2,1,0:T(8,128)(2,1)S(1)}, u32[]{:S(2)}, u32[]{:S(2)}) collective-permute-start(bf16[2,8,16,16,128]{4,3,2,1,0:T(8,128)(2,1)} %get-tuple-element.14.refs_1_), channel_id=1, source_target_pairs={{0,2},{2,4},{4,6},{6,8},{8,10},{10,12},{12,14},{1,3},{3,5},{5,7},{... | collective-permute-start | bytes 3145736 | tf_op jit(solution)/shard_map/ppermute | solution.py:381
  14.8 1.4 %copy.17 = f32[4,2,8,128]{3,2,1,0:T(8,128)} copy(f32[4,2,8,128]{3,1,0,2:T(2,128)} %bitcast.21) | data formatting | bytes 65536 | tf_op jit(solution)/shard_map/transpose | solution.py:422
  16.2 24.7 %stats0.1.refs_2_ = f32[6,2,8,128]{3,2,1,0:T(8,128)} custom-call(f32[4,16,128]{2,1,0:T(8,128)} %bitcast.19, f32[1,128]{1,0:T(1,128)} %bitcast.22), custom_call_target="tpu_custom_call" | custom-call | tf_op jit(solution)/shard_map/stats0/pallas_call | solution.py:136
  40.9 12.2 %firsta.1 = (f32[512,128]{1,0:T(8,128)}, f32[512,128]{1,0:T(8,128)}) custom-call(s32[1]{0:T(128)} %bitcast.2.flag, bf16[2,8,16,16,128]{4,3,2,1,0:T(8,128)(2,1)} %get-tuple-element.15.refs_0_.refs_1_, bf16[2,8,16,16,128]{4,3,2,1,0:T(8,128)(2,1)} %get-tuple-element.14.refs_1_, f32[6,2,8,128]{3,2,1,0:T(8,128)} %stats0.1.refs_2_, f32[1,128]{1,0:T(1,128)} %bitcast.25, ...), custom_call_target="tpu_custom_call" | custom-call | flops 8000000000 | bytes 6000000 | tf_op jit(solution)/shard_map/firsta/pallas_call | solution.py:271
  53.1 2.4 %collective-permute-start.3 = (f32[512,128]{1,0:T(8,128)}, f32[512,128]{1,0:T(8,128)S(1)}, u32[]{:S(2)}, u32[]{:S(2)}) collective-permute-start(f32[512,128]{1,0:T(8,128)} %get-tuple-element.18), channel_id=1, source_target_pairs={{0,2},{2,4},{4,6},{6,8},{8,10},{10,12},{12,14},{1,3},{3,5},{5,7},{... | collective-permute-start | bytes 786440 | tf_op jit(solution)/shard_map/ppermute | solution.py:381
  55.6 2.2 %collective-permute-start = (s32[13]{0:T(128)S(1)}, s32[13]{0:T(128)S(1)}, u32[]{:S(2)}, u32[]{:S(2)}) collective-permute-start(s32[13]{0:T(128)S(1)} %pad_add_fusion), channel_id=1, source_target_pairs={{0,1},{1,0},{2,3},{3,2},{4,5},{5,4},{6,7},{7,6},{8,9},{9,8},{10,11... | collective-permute-start | bytes 164 | tf_op jit(solution)/shard_map/ppermute | solution.py:385
  57.8 4.2 %collective-permute-done.3.refs_7_ = f32[512,128]{1,0:T(8,128)S(1)} collective-permute-done((f32[512,128]{1,0:T(8,128)}, f32[512,128]{1,0:T(8,128)S(1)}, u32[]{:S(2)}, u32[]{:S(2)}) %collective-permute-start.3) | collective-permute-done | bytes 262176 | tf_op jit(solution)/shard_map/ppermute | solution.py:381
  62.0 0.7 copy-done.3
  63.1 12.4 %firstb.1 = (bf16[2,512,128]{2,1,0:T(8,128)(2,1)}, f32[2,16,128]{2,1,0:T(8,128)}) custom-call(s32[1]{0:T(128)} %bitcast.2.flag, bf16[2,8,16,16,128]{4,3,2,1,0:T(8,128)(2,1)} %copy-done.2, bf16[2,8,16,16,128]{4,3,2,1,0:T(8,128)(2,1)} %get-tuple-element.15.refs_0_.refs_1_, f32[6,2,8,128]{3,2,1,0:T(8,128)} %stats0.1.refs_2_, f32[1,128]{1,0:T(1,128)} %bitcast.26, ...), custom_call_target="tpu_custom_call" | custom-call | flops 8000000000 | bytes 6000000 | tf_op jit(solution)/shard_map/firstb/pallas_call | solution.py:271
  75.6 1.9 %collective-permute-start.4 = (bf16[2,512,128]{2,1,0:T(8,128)(2,1)}, bf16[2,512,128]{2,1,0:T(8,128)(2,1)S(1)}, u32[]{:S(2)}, u32[]{:S(2)}) collective-permute-start(bf16[2,512,128]{2,1,0:T(8,128)(2,1)} %get-tuple-element.19.lev_ref), channel_id=1, source_target_pairs={{0,2},{2,4},{4,6},{6,8},{8,10},{10,12},{12,14},{1,3},{3,5},{5,7},{... | collective-permute-start | bytes 786440 | tf_op jit(solution)/shard_map/ppermute | solution.py:381
  79.4 8.6 %stats1.1.p_ref = f32[4,2,8,128]{3,2,1,0:T(8,128)} custom-call(f32[2,16,128]{2,1,0:T(8,128)} %get-tuple-element.20.s_ref, f32[1,128]{1,0:T(1,128)} %bitcast.23), custom_call_target="tpu_custom_call" | custom-call | tf_op jit(solution)/shard_map/stats1/pallas_call | solution.py:136
  88.0 0.7 copy-done.1
  88.7 8.4 %secondk.1 = (f32[128,256]{1,0:T(8,128)}, f32[128,256]{1,0:T(8,128)}) custom-call(s32[1]{0:T(128)} %bitcast.2.flag, bf16[2,512,128]{2,1,0:T(8,128)(2,1)} %copy-done.1, bf16[2,512,128]{2,1,0:T(8,128)(2,1)} %get-tuple-element.19.lev_ref, f32[4,2,8,128]{3,2,1,0:T(8,128)} %stats1.1.p_ref, f32[1,128]{1,0:T(1,128)} %bitcast.24, bf16[3,1152,256]{2,1,0:T(8,128)(2,1)} %bitcast.18, ...), custom_call_target="tpu_custom_call" | custom-call | tf_op jit(solution)/shard_map/secondk/pallas_call | solution.py:358
  97.1 2.6 %collective-permute-start.5 = (f32[128,256]{1,0:T(8,128)}, f32[128,256]{1,0:T(8,128)S(1)}, u32[]{:S(2)}, u32[]{:S(2)}) collective-permute-start(f32[128,256]{1,0:T(8,128)} %get-tuple-element.22), channel_id=1, source_target_pairs={{0,2},{2,4},{4,6},{6,8},{8,10},{10,12},{12,14},{1,3},{3,5},{5,7},{... | collective-permute-start | bytes 393224 | tf_op jit(solution)/shard_map/ppermute | solution.py:381
  99.7 4.1 %collective-permute-done.5 = f32[128,256]{1,0:T(8,128)S(1)} collective-permute-done((f32[128,256]{1,0:T(8,128)}, f32[128,256]{1,0:T(8,128)S(1)}, u32[]{:S(2)}, u32[]{:S(2)}) %collective-permute-start.5) | collective-permute-done | bytes 131104 | tf_op jit(solution)/shard_map/ppermute | solution.py:381
  103.9 0.9 add_convert_fusion
  104.9 4.9 %collective-permute-start.6 = (bf16[8,4096]{1,0:T(8,128)(2,1)S(1)}, bf16[8,4096]{1,0:T(8,128)(2,1)S(1)}, u32[]{:S(2)}, u32[]{:S(2)}) collective-permute-start(bf16[8,4096]{1,0:T(8,128)(2,1)S(1)} %reshape.54), channel_id=1, source_target_pairs={{0,1},{1,0},{2,3},{3,2},{4,5},{5,4},{6,7},{7,6},{8,9},{9,8},{10,11... | collective-permute-start | bytes 196616 | tf_op jit(solution)/shard_map/ppermute | solution.py:385
  109.8 0.8 collective-permute-done.6
  110.8 0.7 copy.15
  (19 shorter events, 2.1 us)
Async XLA Ops:
  1.4 3.0 %collective-permute-start.1 = (bf16[4,4,16,16,128]{4,3,2,1,0:T(8,128)(2,1)S(1)}, bf16[4,4,16,16,128]{4,3,2,1,0:T(8,128)(2,1)S(1)}, u32[]{:S(2)}, u32[]{:S(2)}) collective-permute-start(bf16[4,4,16,16,128]{4,3,2,1,0:T(8,128)(2,1)S(1)} %slice.38), channel_id=1, source_target_pairs={{0,1},{1,0},{2,3},{3,2},{4,5},{5,4},{6,7},{7,6},{8,9},{9,8},{10,11... | collective-permute-start | bytes 3145736 | tf_op jit(solution)/shard_map/ppermute | solution.py:385
  4.4 1.0 copy-start
  11.7 50.4 %collective-permute-start.2 = (bf16[2,8,16,16,128]{4,3,2,1,0:T(8,128)(2,1)}, bf16[2,8,16,16,128]{4,3,2,1,0:T(8,128)(2,1)S(1)}, u32[]{:S(2)}, u32[]{:S(2)}) collective-permute-start(bf16[2,8,16,16,128]{4,3,2,1,0:T(8,128)(2,1)} %get-tuple-element.14.refs_1_), channel_id=1, source_target_pairs={{0,2},{2,4},{4,6},{6,8},{8,10},{10,12},{12,14},{1,3},{3,5},{5,7},{... | collective-permute-start | bytes 3145736 | tf_op jit(solution)/shard_map/ppermute | solution.py:381
  40.9 14.6 %copy-start.4 = (s32[12]{0:T(128)S(1)}, s32[12]{0:T(128)}, u32[]{:S(2)}) copy-start(s32[12]{0:T(128)} %param.14) | copy-start | bytes 148
  53.1 8.9 %collective-permute-start.3 = (f32[512,128]{1,0:T(8,128)}, f32[512,128]{1,0:T(8,128)S(1)}, u32[]{:S(2)}, u32[]{:S(2)}) collective-permute-start(f32[512,128]{1,0:T(8,128)} %get-tuple-element.18), channel_id=1, source_target_pairs={{0,2},{2,4},{4,6},{6,8},{8,10},{10,12},{12,14},{1,3},{3,5},{5,7},{... | collective-permute-start | bytes 786440 | tf_op jit(solution)/shard_map/ppermute | solution.py:381
  55.6 21.9 %collective-permute-start = (s32[13]{0:T(128)S(1)}, s32[13]{0:T(128)S(1)}, u32[]{:S(2)}, u32[]{:S(2)}) collective-permute-start(s32[13]{0:T(128)S(1)} %pad_add_fusion), channel_id=1, source_target_pairs={{0,1},{1,0},{2,3},{3,2},{4,5},{5,4},{6,7},{7,6},{8,9},{9,8},{10,11... | collective-permute-start | bytes 164 | tf_op jit(solution)/shard_map/ppermute | solution.py:385
  62.0 0.7 copy-start.3
  62.0 1.1 copy-start.2
  75.6 12.4 %collective-permute-start.4 = (bf16[2,512,128]{2,1,0:T(8,128)(2,1)}, bf16[2,512,128]{2,1,0:T(8,128)(2,1)S(1)}, u32[]{:S(2)}, u32[]{:S(2)}) collective-permute-start(bf16[2,512,128]{2,1,0:T(8,128)(2,1)} %get-tuple-element.19.lev_ref), channel_id=1, source_target_pairs={{0,2},{2,4},{4,6},{6,8},{8,10},{10,12},{12,14},{1,3},{3,5},{5,7},{... | collective-permute-start | bytes 786440 | tf_op jit(solution)/shard_map/ppermute | solution.py:381
  88.0 0.7 copy-start.1
  97.1 6.8 %collective-permute-start.5 = (f32[128,256]{1,0:T(8,128)}, f32[128,256]{1,0:T(8,128)S(1)}, u32[]{:S(2)}, u32[]{:S(2)}) collective-permute-start(f32[128,256]{1,0:T(8,128)} %get-tuple-element.22), channel_id=1, source_target_pairs={{0,2},{2,4},{4,6},{6,8},{8,10},{10,12},{12,14},{1,3},{3,5},{5,7},{... | collective-permute-start | bytes 393224 | tf_op jit(solution)/shard_map/ppermute | solution.py:381
  104.9 5.8 %collective-permute-start.6 = (bf16[8,4096]{1,0:T(8,128)(2,1)S(1)}, bf16[8,4096]{1,0:T(8,128)(2,1)S(1)}, u32[]{:S(2)}, u32[]{:S(2)}) collective-permute-start(bf16[8,4096]{1,0:T(8,128)(2,1)S(1)} %reshape.54), channel_id=1, source_target_pairs={{0,1},{1,0},{2,3},{3,2},{4,5},{5,4},{6,7},{7,6},{8,9},{9,8},{10,11... | collective-permute-start | bytes 196616 | tf_op jit(solution)/shard_map/ppermute | solution.py:385

commit v2 on v0

v2 whole, which is shorter than its diff:
```python
import functools

import jax
import jax.numpy as jnp
import numpy as np
from jax import lax
from jax.experimental import pallas as pl
from jax.experimental.pallas import tpu as pltpu
from jax.sharding import PartitionSpec as P

GROUPS = 32
OWN = 8
MOVED = 4
EPS = 1e-06
F32 = jnp.float32
BF16 = jnp.bfloat16
MESH = pl.DeviceIdType.MESH
VMEM = pl.BlockSpec(memory_space=pltpu.VMEM)
LIMIT = 56 << 20


def full(shape):
    return pl.BlockSpec(shape, lambda j, *_: (0,) * len(shape))


def prep_kernel(flag, own_ref, recv_ref, xa_ref, xb_ref, sums_ref):
    j = pl.program_id(0)
    keep = jnp.logical_or(j < OWN - MOVED, flag[0] == 1)

    def put(ref):
        for f in range(4):
            v = ref[f, 0]
            out = xa_ref if f < 2 else xb_ref
            out[f % 2, 0] = v
            w = v.astype(F32).reshape(256, 128)
            sums_ref[f, pl.ds(j, 1)] = jnp.sum(w, axis=0, keepdims=True)
            sums_ref[f, pl.ds(OWN + j, 1)] = jnp.sum(w * w, axis=0, keepdims=True)

    @pl.when(keep)
    def _():
        put(own_ref)

    @pl.when(jnp.logical_not(keep))
    def _():
        put(recv_ref)


def prep(acts, recv, flag):
    cells = acts.shape[2:]
    block = (4, 1) + cells
    pair = (2, 1) + cells
    return pl.pallas_call(
        prep_kernel,
        out_shape=(
            jax.ShapeDtypeStruct((2, OWN) + cells, BF16),
            jax.ShapeDtypeStruct((2, OWN) + cells, BF16),
            jax.ShapeDtypeStruct((4, 2 * OWN, 128), F32),
        ),
        grid_spec=pltpu.PrefetchScalarGridSpec(
            num_scalar_prefetch=1,
            grid=(OWN,),
            in_specs=[
                pl.BlockSpec(block, lambda j, f: (0, jnp.where(f[0] == 1, j, jnp.minimum(j, MOVED - 1)), 0, 0, 0)),
                pl.BlockSpec(block, lambda j, f: (0, jnp.where(f[0] == 1, 0, jnp.maximum(j - MOVED, 0)), 0, 0, 0)),
            ],
            out_specs=[
                pl.BlockSpec(pair, lambda j, f: (0, j, 0, 0, 0)),
                pl.BlockSpec(pair, lambda j, f: (0, j, 0, 0, 0)),
                full((4, 2 * OWN, 128)),
            ],
        ),
        name="prep",
        compiler_params=pltpu.CompilerParams(vmem_limit_bytes=LIMIT),
    )(flag, acts, recv)


def silu(u):
    return (0.5 * u) * (1.0 + jnp.tanh(0.5 * u))


def shifted(v, side):
    rows = v.shape[0]
    col = lax.broadcasted_iota(jnp.int32, v.shape, 0) % side
    left = jnp.where(col == 0, 0.0, pltpu.roll(v, 1, axis=0))
    right = jnp.where(col == side - 1, 0.0, pltpu.roll(v, rows - 1, axis=0))
    return left, right


def pick_matrix():
    m = np.zeros((9, OWN, 4, 4, OWN, 8, 8), np.float32)
    for b in range(3):
        for c in range(3):
            for y in range(4):
                for x in range(4):
                    h, w = 2 * y + b - 1, 2 * x + c - 1
                    if 0 <= h < 8 and 0 <= w < 8:
                        for t in range(OWN):
                            m[b * 3 + c, t, y, x, t, h, w] = 1.0
    return m.reshape(9 * OWN * 16, OWN * 64)


def main_kernel(
    n,
    per_frame,
    xa_ref,
    xb_ref,
    s_ref,
    gain1_ref,
    shift1_ref,
    conv1_ref,
    down1_ref,
    gain2_ref,
    shift2_ref,
    conv2_ref,
    short_ref,
    down2_ref,
    pick_ref,
    out_ref,
    mine1,
    got1,
    mine2,
    got2,
    p1,
    p2,
    halo,
    buf,
    w2,
    wd,
    sf,
    lhs,
    own1,
    next1,
    part1,
    level,
    lhalo,
    lhs2,
    own2,
    next2,
    part2,
    enc,
    renc,
    send1,
    recv1,
    send2,
    recv2,
    sems,
):
    me = lax.axis_index("tm")
    right = lax.rem(me + 1, n)
    partner = 1 - lax.axis_index("tile")
    barrier = pltpu.get_barrier_semaphore()
    for k in range(1, n):
        pl.semaphore_signal(barrier, inc=1, device_id={"tm": lax.rem(me + k, n)}, device_id_type=MESH)
    pl.semaphore_signal(barrier, inc=1, device_id={"tile": partner}, device_id_type=MESH)

    def to_right(src, dst, i):
        return pltpu.make_async_remote_copy(
            src_ref=src,
            dst_ref=dst,
            send_sem=sems.at[2 * i],
            recv_sem=sems.at[2 * i + 1],
            device_id={"tm": right},
            device_id_type=MESH,
        )

    def send(copy):
        @pl.when(me < n - 1)
        def _():
            copy.start()

    def sent(copy):
        @pl.when(me < n - 1)
        def _():
            copy.wait_send()

    def landed(copy):
        @pl.when(me > 0)
        def _():
            copy.wait_recv()

    def fill(sums, mine):
        partial = sums[0]
        for f in range(1, len(sums) - 1):
            partial = partial + sums[f]
        mine[1] = partial
        mine[0] = partial + sums[-1]

    def share(mine, got, send_sem, recv_sem):
        copies = []
        for k in range(1, n):
            src, dst = (mine, got.at[k]) if k == 1 else (mine.at[0], got.at[k, 0])
            c = pltpu.make_async_remote_copy(
                src_ref=src,
                dst_ref=dst,
                send_sem=send_sem.at[k],
                recv_sem=recv_sem.at[k],
                device_id={"tm": lax.rem(me + k, n)},
                device_id_type=MESH,
            )
            c.start()
            copies.append(c)
        return copies

    def norms(sums, copies, got, gain, size, out):
        frames = len(sums)
        rest = jnp.zeros_like(sums[0])
        for k in range(n - 1, 1, -1):
            copies[k - 1].wait()
            rest = rest + jnp.where(k <= me, got[k, 0], 0.0)
        copies[0].wait()
        before = rest + jnp.where(me >= 1, got[1, 0], 0.0)
        rows = [rest + jnp.where(me >= 1, got[1, 1], 0.0), before]
        run = before
        for f in range(frames):
            run = run + sums[f]
            rows.append(run)
        ri = lax.broadcasted_iota(jnp.int32, (128, 128), 0) // (128 // GROUPS)
        ci = lax.broadcasted_iota(jnp.int32, (128, 128), 1) // (128 // GROUPS)
        same = jnp.where(ri == ci, 1.0, 0.0).astype(F32)
        grouped = jnp.dot(
            jnp.concatenate(rows, axis=0), same, precision=lax.Precision.HIGHEST, preferred_element_type=F32
        )
        start = (me * frames).astype(F32)
        made = []
        for i in range(frames + 2):
            count = jnp.maximum(start + float(i - 1), 1.0) * size
            inv_count = jnp.full((1, 128), 1.0, F32) / (jnp.zeros((1, 128), F32) + count)
            g = grouped[i * 2 * OWN : (i + 1) * 2 * OWN]
            m = g[0:OWN] * inv_count
            var = g[OWN : 2 * OWN] * inv_count - m * m
            made.append((m, lax.rsqrt(var + EPS) * gain[...]))
        for i in range(frames + 2):
            for z in range(2):
                v = made[i][z]
                out[i, z] = jnp.where(me == 0, made[2][z], v) if i < 2 else v

    sums1 = [s_ref[f] for f in range(4)]
    fill(sums1, mine1)
    pl.semaphore_wait(barrier, n)
    copies1 = share(mine1, got1, send1, recv1)

    zero = jnp.zeros((128, 128), BF16)
    for q in range(4):
        for b in range(3):
            for c in range(3):
                for e in range(2):
                    a = q - e
                    k = (q % 2) * 384 + c * 128
                    w2[(q // 2) * 3 + b, k : k + 128, e * 128 : e * 128 + 128] = (
                        conv1_ref[a, b, c] if 0 <= a < 3 else zero
                    )
    for b in range(3):
        for c in range(3):
            wd[b, c * 128 : c * 128 + 128, 0:128] = down1_ref[2, b, c]
            wd[b, 384 + c * 128 : 512 + c * 128, 0:128] = zero
            wd[b, c * 128 : c * 128 + 128, 128:256] = down1_ref[0, b, c]
            wd[b, 384 + c * 128 : 512 + c * 128, 128:256] = down1_ref[1, b, c]
    edge = jnp.zeros((16, 768), BF16)
    for p in range(2):
        buf[p, 0:16] = edge
        buf[p, 272:288] = edge

    norms(sums1, copies1, got1, gain1_ref, per_frame, p1)
    halo_copy = to_right(xb_ref, halo, 0)
    send(halo_copy)

    def first_tiles(base, ra, rb):
        def step(j, _):
            for q in range(4):
                x = (ra if q < 2 else rb)[q % 2, j].astype(F32).reshape(256, 128)
                mean = p1[base + q, 0, pl.ds(j, 1), :]
                scale = p1[base + q, 1, pl.ds(j, 1), :]
                h = silu((x - mean) * scale + shift1_ref[...])
                left, right_ = shifted(h, 16)
                k = (q % 2) * 384
                buf[q // 2, 16:272, k : k + 128] = left.astype(BF16)
                buf[q // 2, 16:272, k + 128 : k + 256] = h.astype(BF16)
                buf[q // 2, 16:272, k + 256 : k + 384] = right_.astype(BF16)
            acc = jnp.zeros((256, 256), F32)
            for p in range(2):
                for b in range(3):
                    acc = acc + jnp.dot(
                        buf[p, b * 16 : b * 16 + 256, :], w2[p * 3 + b], preferred_element_type=F32
                    )
            for e in range(2):
                x = rb[e, j].astype(F32).reshape(256, 128)
                sf[e] = (x + acc[:, e * 128 : e * 128 + 128]).astype(BF16).astype(F32)
            row = pl.multiple_of(j * 64, 64)
            col = lax.broadcasted_iota(jnp.int32, (128, 128), 0) % 8
            for e in range(2):
                even = sf[e, pl.ds(0, 128, stride=2), :]
                odd = sf[e, pl.ds(1, 128, stride=2), :]
                prev = jnp.where(col == 0, 0.0, pltpu.roll(odd, 1, axis=0))
                for c, v in enumerate((prev, even, odd)):
                    v = v.reshape(8, 2, 8, 128)
                    top, low = v[:, 0], v[:, 1]
                    up = jnp.concatenate([jnp.zeros((1, 8, 128), F32), low[:7]], axis=0)
                    k = e * 384 + c * 128
                    for b, u in enumerate((up, top, low)):
                        lhs[b, pl.ds(row, 64), k : k + 128] = u.reshape(64, 128).astype(BF16)
            return 0

        lax.fori_loop(0, OWN, step, 0)
        out = jnp.zeros((512, 256), F32)
        for b in range(3):
            out = out + jnp.dot(lhs[b], wd[b], preferred_element_type=F32)
        return out

    out = first_tiles(2, xa_ref, xb_ref)
    own1[...] = out[:, 0:128]
    next1[...] = out[:, 128:256]
    part_copy = to_right(next1, part1, 1)
    send(part_copy)

    @pl.when(me == 0)
    def _():
        halo[0] = xa_ref[0]
        halo[1] = xa_ref[0]

    landed(halo_copy)
    out = first_tiles(0, halo, xa_ref)
    level[1] = (own1[...] + out[:, 128:256]).astype(BF16)
    own1[...] = out[:, 0:128]

    @pl.when(me == 0)
    def _():
        extra = jnp.zeros((512, 128), F32)
        for b in range(3):
            twice = jnp.concatenate([lhs[b, :, 0:384], lhs[b, :, 0:384]], axis=1)
            extra = extra + jnp.dot(twice, wd[b, :, 128:256], preferred_element_type=F32)
        part1[...] = extra

    landed(part_copy)
    level[0] = (own1[...] + part1[...]).astype(BF16)
    sent(halo_copy)
    sent(part_copy)

    sums2 = []
    for f in range(2):
        v = level[f].astype(F32).reshape(OWN, 64, 128)
        sums2.append(jnp.concatenate([jnp.sum(v, axis=1), jnp.sum(v * v, axis=1)], axis=0))
    fill(sums2, mine2)
    copies2 = share(mine2, got2, send2, recv2)
    lhalo_copy = to_right(level, lhalo, 2)
    send(lhalo_copy)

    @pl.when(me == 0)
    def _():
        lhalo[0] = level[0]
        lhalo[1] = level[0]

    norms(sums2, copies2, got2, gain2_ref, per_frame / 4, p2)

    def second_tiles(base, ref):
        def step(t, _):
            rows = pl.ds(pl.multiple_of(t * 64, 64), 64)
            for q in range(2):
                x = ref[q, rows, :].astype(F32)
                mean = p2[base + q, 0, pl.ds(t, 1), :]
                scale = p2[base + q, 1, pl.ds(t, 1), :]
                h = silu((x - mean) * scale + shift2_ref[...])
                left, right_ = shifted(h, 8)
                pad = jnp.zeros((8, 128), F32)
                for c, v in enumerate((left, h, right_)):
                    up = jnp.concatenate([pad, v[:56]], axis=0)
                    low = jnp.concatenate([v[8:], pad], axis=0)
                    for b, u in enumerate((up, v, low)):
                        k = (b * 3 + c) * 128
                        lhs2[base + q, rows, k : k + 128] = u.astype(BF16)
            return 0

        lax.fori_loop(0, OWN, step, 0)

    second_tiles(2, level)
    landed(lhalo_copy)
    second_tiles(0, lhalo)
    level2 = []
    for f in range(2):
        acc = jnp.dot(level[f], short_ref[...], preferred_element_type=F32)
        for a in range(3):
            acc = acc + jnp.dot(lhs2[f + a], conv2_ref[a], preferred_element_type=F32)
        level2.append(acc.astype(BF16))
    own = jnp.zeros((128, 256), F32)
    nxt = jnp.zeros((128, 256), F32)
    for i in range(9):
        pick = pick_ref[i * 128 : i * 128 + 128]
        s0 = jnp.dot(pick, level2[0], preferred_element_type=F32).astype(BF16)
        s1 = jnp.dot(pick, level2[1], preferred_element_type=F32).astype(BF16)
        own = own + jnp.dot(s0, down2_ref[18 + i], preferred_element_type=F32)
        nxt = nxt + jnp.dot(s0, down2_ref[i], preferred_element_type=F32)
        nxt = nxt + jnp.dot(s1, down2_ref[9 + i], preferred_element_type=F32)
        lhs2[0, 0:128, i * 128 : i * 128 + 128] = s0[:, 0:128]
        lhs2[1, 0:128, i * 128 : i * 128 + 128] = s0[:, 128:256]
    next2[...] = nxt
    part2_copy = to_right(next2, part2, 3)
    send(part2_copy)
    own2[...] = own

    @pl.when(me == 0)
    def _():
        extra = jnp.zeros((128, 256), F32)
        for i in range(9):
            s0 = jnp.concatenate(
                [lhs2[0, 0:128, i * 128 : i * 128 + 128], lhs2[1, 0:128, i * 128 : i * 128 + 128]], axis=1
            )
            extra = extra + jnp.dot(s0, down2_ref[i], preferred_element_type=F32)
            extra = extra + jnp.dot(s0, down2_ref[9 + i], preferred_element_type=F32)
        part2[...] = extra

    landed(part2_copy)
    enc[...] = (own2[...] + part2[...]).astype(BF16)
    swap = pltpu.make_async_remote_copy(
        src_ref=enc,
        dst_ref=renc,
        send_sem=sems.at[8],
        recv_sem=sems.at[9],
        device_id={"tile": partner},
        device_id_type=MESH,
    )
    swap.start()
    out_ref[0] = enc[...]
    sent(lhalo_copy)
    sent(part2_copy)
    swap.wait()
    out_ref[1] = renc[...]


def encode(xa, xb, sums, params, n):
    (
        first_gain,
        first_shift,
        first_conv,
        first_down,
        second_gain,
        second_shift,
        second_conv,
        second_short,
        second_down,
    ) = params
    cells = xa.shape[2:]
    rows = OWN * 64
    vm = pltpu.VMEM
    line = lambda v: v.reshape(1, 128)
    return pl.pallas_call(
        functools.partial(main_kernel, n, float(cells[0] * cells[1] * (cells[2] // GROUPS))),
        out_shape=jax.ShapeDtypeStruct((2, OWN * 16, 256), BF16),
        in_specs=[VMEM] * 13,
        out_specs=VMEM,
        scratch_shapes=[
            vm((2, 2 * OWN, 128), F32),
            vm((n, 2, 2 * OWN, 128), F32),
            vm((2, 2 * OWN, 128), F32),
            vm((n, 2, 2 * OWN, 128), F32),
            vm((6, 2, OWN, 128), F32),
            vm((4, 2, OWN, 128), F32),
            vm((2, OWN) + cells, BF16),
            vm((2, 288, 768), BF16),
            vm((6, 768, 256), BF16),
            vm((3, 768, 256), BF16),
            vm((2, 256, 128), F32),
            vm((3, rows, 768), BF16),
            vm((rows, 128), F32),
            vm((rows, 128), F32),
            vm((rows, 128), F32),
            vm((2, rows, 128), BF16),
            vm((2, rows, 128), BF16),
            vm((4, rows, 1152), BF16),
            vm((OWN * 16, 256), F32),
            vm((OWN * 16, 256), F32),
            vm((OWN * 16, 256), F32),
            vm((OWN * 16, 256), BF16),
            vm((OWN * 16, 256), BF16),
            pltpu.SemaphoreType.DMA((n,)),
            pltpu.SemaphoreType.DMA((n,)),
            pltpu.SemaphoreType.DMA((n,)),
            pltpu.SemaphoreType.DMA((n,)),
            pltpu.SemaphoreType.DMA((10,)),
        ],
        name="encode",
        compiler_params=pltpu.CompilerParams(collective_id=0, has_side_effects=True, vmem_limit_bytes=LIMIT),
    )(
        xa,
        xb,
        sums,
        line(first_gain),
        line(first_shift),
        first_conv,
        first_down,
        line(second_gain),
        line(second_shift),
        second_conv.reshape(3, 1152, 256),
        second_short,
        second_down.reshape(27, 256, 256),
        jnp.asarray(pick_matrix(), BF16),
    )


def swapped(value):
    return lax.ppermute(value, "tile", [(0, 1), (1, 0)])


def body(
    activations,
    tile_ids,
    tile_counts,
    first_gain,
    first_shift,
    first_conv,
    first_down,
    second_gain,
    second_shift,
    second_conv,
    second_short,
    second_down,
):
    n = lax.axis_size("tm")
    me = lax.axis_index("tile")
    cap = activations.shape[1]
    recv = swapped(activations[:, OWN:cap])
    info = jnp.concatenate([tile_ids, tile_counts])
    other = swapped(info)
    heavy = (tile_counts[0] == cap).astype(jnp.int32).reshape(1)

    def encoded_ids(a, b):
        slots = jnp.arange(cap)
        ids_a = jnp.where(slots < a[cap], a[:cap], -1)
        ids_b = jnp.where(slots < b[cap], b[:cap], -1)
        kept = jnp.where(a[cap] == cap, ids_a[OWN - MOVED : OWN], ids_b[OWN:])
        return jnp.concatenate([ids_a[: OWN - MOVED], kept])

    ids = jnp.concatenate([encoded_ids(info, other), encoded_ids(other, info)])

    xa, xb, sums = prep(activations, recv, heavy)
    params = (
        first_gain,
        first_shift,
        first_conv,
        first_down,
        second_gain,
        second_shift,
        second_conv,
        second_short,
        second_down,
    )
    both = encode(xa, xb, sums, params, n).reshape(2 * OWN, 16 * 256)
    select = (ids[None, :] == (me * OWN + jnp.arange(OWN))[:, None]).astype(BF16)
    latents = jnp.dot(select, both, preferred_element_type=F32).astype(BF16)
    return latents.reshape(1, OWN, 4, 4, 256)


def solution(mesh):
    placed = (
        P(("groups", "tm"), "tile", None, None, None),
        P(("groups", "tile")),
        P(("groups", "tile")),
    ) + (P(),) * 9
    return jax.shard_map(
        body,
        mesh=mesh,
        in_specs=placed,
        out_specs=P(("groups", "tm"), "tile", None, None, None),
        check_vma=False,
    )
```

time: 349 us -> 78.5 us (0.22); the launches traced: 343 us -> 77.8 us
  blocking collectives: 132 us -> 0 us
  Pallas kernels: 0 us -> 68.3 us
  waiting for transfers between devices: 51.3 us -> 0.45 us
  other arithmetic: 51.9 us -> 2.19 us
  matrix products: 47 us -> 0.21 us
  local copies, waits for them, and re-layouts: 40.9 us -> 4.62 us
  starting transfers between devices: 19.8 us -> 0.75 us
    all_gather x4 -> x0, blocking collectives: 98 us -> none  [prefix(): everything = jax.tree.map(lambda part: lax.all_gather(part, axis), shard)]
    pallas_call x0 -> x2, Pallas kernels: none -> 68.3 us  [the longest x1 62.2 us: encode(): pl.pallas_call(functools.partial(main_kernel, n, float(cells[0] * cells[1...]
    ppermute x4 -> x2, waiting for transfers between devices: 51.3 us -> 0.45 us  [swapped(): return lax.ppermute(value, 'tile', [(0, 1), (1, 0)])]
    conv_general_dilated x3 -> x0, matrix products: 42.2 us -> none  [causal_conv(): lax.conv_general_dilated(padded, kernel, (stride, stride, stride), ((0, 0...]
    all_to_all x1 -> x0, blocking collectives: 33.5 us -> none  [body(): lax.all_to_all(routed, 'tile', split_axis=1, concat_axis=1, tiled=True)]
    reduce_sum x9 -> x0, other arithmetic: 19.7 us -> none  [the longest x3 10.1 us: normed_cache(): jnp.sum(frame_square, axis=0)]
    ppermute x4 -> x2, starting transfers between devices: 19.8 us -> 0.75 us  [swapped(): return lax.ppermute(value, 'tile', [(0, 1), (1, 0)])]
    select_n x20 -> x3, other arithmetic: 18.9 us -> 1.38 us  [the longest x1 0.66 us: encoded_ids(): ids_a = jnp.where(slots < a[cap], a[:cap], -1)]
  transfers between devices with their start and end apart: 4 -> 2, of which waited for: 4 -> 1; matrix products, arithmetic and copies ran while one was open for 1% -> 4% of each run, Pallas kernels for 0% -> 0%
where the time goes in v2:
time: 78.5 us; the launch traced here: 77.8 us
  Pallas kernels  68.3 us (87%)
  local copies, waits for them, and re-layouts  4.62 us (6%)
  other arithmetic  2.19 us (3%)
  between operations  1.34 us (2%)
    pallas_call x1, Pallas kernels, encode(): pl.pallas_call(functools.partial(main_kernel, n, float(cells[0] * cells[1...  62.2 us
    pallas_call x1, Pallas kernels, prep(): pl.pallas_call(prep_kernel, out_shape=(jax.ShapeDtypeStruct((2, OWN) + ce...  6.07 us
  transfers between devices with their start and end apart: 2, of which 1 were waited for; matrix products, arithmetic and copies ran while one was open for 4% of the time, Pallas kernels for 0%

profile of v2, /device:TPU:17, one launch (start us, length us, event | category | flops | bytes accessed | tf_op | source)
XLA Modules:
  0.0 77.8 jit_solution(14962972428926041699)
XLA Ops:
  0.0 1.4 %slice.38 = bf16[4,4,16,16,128]{4,3,2,1,0:T(8,128)(2,1)S(1)} slice(bf16[4,12,16,16,128]{4,3,2,1,0:T(8,128)(2,1)} %own_ref.1), slice={[0:4], [8:12], [0:16], [0:16], [0:128]} | slice | bytes 2097152 | tf_op jit(solution)/shard_map/slice | solution.py:519
  1.4 0.7 collective-permute-start.1
  2.8 0.7 pad_add_fusion
  3.5 0.0 collective-permute-start
  3.5 0.7 compare_select_fusion.1
  4.2 0.5 collective-permute-done
  4.7 0.6 slice.32
  5.9 0.6 compare_select_fusion
  6.5 0.1 broadcast_select_fusion.1
  6.6 0.1 pad_add_fusion.1
  6.7 0.0 collective-permute-done.1.recv_ref
  6.7 0.0 copy-start
  6.7 1.0 %copy-done = bf16[4,4,16,16,128]{4,3,2,1,0:T(8,128)(2,1)} copy-done((bf16[4,4,16,16,128]{4,3,2,1,0:T(8,128)(2,1)}, bf16[4,4,16,16,128]{4,3,2,1,0:T(8,128)(2,1)S(1)}, u32[]{:S(2)}) %copy-start) | copy-done | bytes 1048600
  7.7 6.1 %prep.1 = (bf16[2,8,16,16,128]{4,3,2,1,0:T(8,128)(2,1)}, bf16[2,8,16,16,128]{4,3,2,1,0:T(8,128)(2,1)}, f32[4,16,128]{2,1,0:T(8,128)}) custom-call(s32[1]{0:T(128)} %bitcast.2.flag, bf16[4,12,16,16,128]{4,3,2,1,0:T(8,128)(2,1)} %own_ref.1, bf16[4,4,16,16,128]{4,3,2,1,0:T(8,128)(2,1)} %copy-done), custom_call_target="tpu_custom_call" | custom-call | tf_op jit(solution)/shard_map/prep/pallas_call | solution.py:52
  13.8 62.2 %encode.1 = bf16[2,128,256]{2,1,0:T(8,128)(2,1)} custom-call(bf16[2,8,16,16,128]{4,3,2,1,0:T(8,128)(2,1)} %get-tuple-element.8.xa_ref, bf16[2,8,16,16,128]{4,3,2,1,0:T(8,128)(2,1)} %get-tuple-element.9.xb_ref, f32[4,16,128]{2,1,0:T(8,128)} %get-tuple-element.10.s_ref, f32[1,128]{1,0:T(1,128)} %bitcast.16, f32[1,128]{1,0:T(1,128)} %bitcast.17, ...), custom_call_target="tpu_custom_call" | custom-call | tf_op jit(solution)/shard_map/encode/pallas_call | solution.py:444
  76.0 1.0 %reshape.42 = bf16[16,4096]{1,0:T(8,128)(2,1)S(1)} reshape(bf16[2,128,256]{2,1,0:T(8,128)(2,1)} %encode.1) | data formatting | bytes 262144 | tf_op jit(solution)/shard_map/reshape | solution.py:545
  77.0 0.2 convolution_convert_fusion
  77.2 0.7 copy.14
  (1 shorter events, 0.0 us)
Async XLA Ops:
  1.4 5.3 %collective-permute-start.1 = (bf16[4,4,16,16,128]{4,3,2,1,0:T(8,128)(2,1)S(1)}, bf16[4,4,16,16,128]{4,3,2,1,0:T(8,128)(2,1)S(1)}, u32[]{:S(2)}, u32[]{:S(2)}) collective-permute-start(bf16[4,4,16,16,128]{4,3,2,1,0:T(8,128)(2,1)S(1)} %slice.38), channel_id=1, source_target_pairs={{0,1},{1,0},{2,3},{3,2},{4,5},{5,4},{6,7},{7,6},{8,9},{9,8},{10,11... | collective-permute-start | bytes 3145736 | tf_op jit(solution)/shard_map/ppermute | solution.py:499
  3.5 1.1 %collective-permute-start = (s32[13]{0:T(128)S(1)}, s32[13]{0:T(128)S(1)}, u32[]{:S(2)}, u32[]{:S(2)}) collective-permute-start(s32[13]{0:T(128)S(1)} %pad_add_fusion), channel_id=1, source_target_pairs={{0,1},{1,0},{2,3},{3,2},{4,5},{5,4},{6,7},{7,6},{8,9},{9,8},{10,11... | collective-permute-start | bytes 164 | tf_op jit(solution)/shard_map/ppermute | solution.py:499
  6.7 1.0 %copy-start = (bf16[4,4,16,16,128]{4,3,2,1,0:T(8,128)(2,1)}, bf16[4,4,16,16,128]{4,3,2,1,0:T(8,128)(2,1)S(1)}, u32[]{:S(2)}) copy-start(bf16[4,4,16,16,128]{4,3,2,1,0:T(8,128)(2,1)S(1)} %collective-permute-done.1.recv_ref) | copy-start | bytes 3145732

commit v3 on v2

--- a/solution.py
+++ b/solution.py
@@ -16,62 +16,8 @@
 BF16 = jnp.bfloat16
 MESH = pl.DeviceIdType.MESH
 VMEM = pl.BlockSpec(memory_space=pltpu.VMEM)
+ANY = pl.BlockSpec(memory_space=pl.ANY)
 LIMIT = 56 << 20
-
-
-def full(shape):
-    return pl.BlockSpec(shape, lambda j, *_: (0,) * len(shape))
-
-
-def prep_kernel(flag, own_ref, recv_ref, xa_ref, xb_ref, sums_ref):
-    j = pl.program_id(0)
-    keep = jnp.logical_or(j < OWN - MOVED, flag[0] == 1)
-
-    def put(ref):
-        for f in range(4):
-            v = ref[f, 0]
-            out = xa_ref if f < 2 else xb_ref
-            out[f % 2, 0] = v
-            w = v.astype(F32).reshape(256, 128)
-            sums_ref[f, pl.ds(j, 1)] = jnp.sum(w, axis=0, keepdims=True)
-            sums_ref[f, pl.ds(OWN + j, 1)] = jnp.sum(w * w, axis=0, keepdims=True)
-
-    @pl.when(keep)
-    def _():
-        put(own_ref)
-
-    @pl.when(jnp.logical_not(keep))
-    def _():
-        put(recv_ref)
-
-
-def prep(acts, recv, flag):
-    cells = acts.shape[2:]
-    block = (4, 1) + cells
-    pair = (2, 1) + cells
-    return pl.pallas_call(
-        prep_kernel,
-        out_shape=(
-            jax.ShapeDtypeStruct((2, OWN) + cells, BF16),
-            jax.ShapeDtypeStruct((2, OWN) + cells, BF16),
-            jax.ShapeDtypeStruct((4, 2 * OWN, 128), F32),
-        ),
-        grid_spec=pltpu.PrefetchScalarGridSpec(
-            num_scalar_prefetch=1,
-            grid=(OWN,),
-            in_specs=[
-                pl.BlockSpec(block, lambda j, f: (0, jnp.where(f[0] == 1, j, jnp.minimum(j, MOVED - 1)), 0, 0, 0)),
-                pl.BlockSpec(block, lambda j, f: (0, jnp.where(f[0] == 1, 0, jnp.maximum(j - MOVED, 0)), 0, 0, 0)),
-            ],
-            out_specs=[
-                pl.BlockSpec(pair, lambda j, f: (0, j, 0, 0, 0)),
-                pl.BlockSpec(pair, lambda j, f: (0, j, 0, 0, 0)),
-                full((4, 2 * OWN, 128)),
-            ],
-        ),
-        name="prep",
-        compiler_params=pltpu.CompilerParams(vmem_limit_bytes=LIMIT),
-    )(flag, acts, recv)
 
 
 def silu(u):
@@ -102,20 +48,26 @@
 def main_kernel(
     n,
     per_frame,
-    xa_ref,
-    xb_ref,
-    s_ref,
+    act_ref,
+    info_ref,
     gain1_ref,
     shift1_ref,
     conv1_ref,
     down1_ref,
     gain2_ref,
     shift2_ref,
+    conv2_hbm,
+    short_ref,
+    down2_hbm,
+    pick_hbm,
+    out_ref,
+    x,
+    moved,
+    rinfo,
+    s_ref,
     conv2_ref,
-    short_ref,
     down2_ref,
     pick_ref,
-    out_ref,
     mine1,
     got1,
     mine2,
@@ -144,9 +96,14 @@
     send2,
     recv2,
     sems,
+    hsend,
+    hrecv,
+    local,
 ):
     me = lax.axis_index("tm")
     right = lax.rem(me + 1, n)
+    fetch = pltpu.make_async_copy(act_ref.at[:, 0:OWN], x, local.at[0])
+    fetch.start()
     partner = 1 - lax.axis_index("tile")
     barrier = pltpu.get_barrier_semaphore()
     for k in range(1, n):
@@ -234,11 +191,26 @@
                 v = made[i][z]
                 out[i, z] = jnp.where(me == 0, made[2][z], v) if i < 2 else v
 
-    sums1 = [s_ref[f] for f in range(4)]
-    fill(sums1, mine1)
     pl.semaphore_wait(barrier, n)
-    copies1 = share(mine1, got1, send1, recv1)
-
+
+    def swap(src, dst, i):
+        return pltpu.make_async_remote_copy(
+            src_ref=src,
+            dst_ref=dst,
+            send_sem=sems.at[2 * i],
+            recv_sem=sems.at[2 * i + 1],
+            device_id={"tile": partner},
+            device_id_type=MESH,
+        )
+
+    move_copy = swap(act_ref.at[:, OWN : OWN + MOVED], moved, 5)
+    move_copy.start()
+    info_copy = swap(info_ref, rinfo, 6)
+    info_copy.start()
+    late = [
+        pltpu.make_async_copy(a, b, local.at[1 + i])
+        for i, (a, b) in enumerate(((conv2_hbm, conv2_ref), (down2_hbm, down2_ref), (pick_hbm, pick_ref)))
+    ]
     zero = jnp.zeros((128, 128), BF16)
     for q in range(4):
         for b in range(3):
@@ -256,40 +228,92 @@
             wd[b, c * 128 : c * 128 + 128, 128:256] = down1_ref[0, b, c]
             wd[b, 384 + c * 128 : 512 + c * 128, 128:256] = down1_ref[1, b, c]
     edge = jnp.zeros((16, 768), BF16)
-    for p in range(2):
-        buf[p, 0:16] = edge
-        buf[p, 272:288] = edge
-
+    for z in range(2):
+        for p in range(2):
+            buf[z, p, 0:16] = edge
+            buf[z, p, 272:288] = edge
+
+    heavy = info_ref[2:3, :] == 1
+
+    def add_up(f, j, v):
+        s_ref[f, pl.ds(j, 1), :] = jnp.sum(v, axis=0, keepdims=True)
+        s_ref[f, pl.ds(OWN + j, 1), :] = jnp.sum(v * v, axis=0, keepdims=True)
+
+    fetch.wait()
+
+    def count_own(j, _):
+        for f in range(4):
+            add_up(f, j, x[f, j].astype(F32).reshape(256, 128))
+        return 0
+
+    lax.fori_loop(0, OWN - MOVED, count_own, 0)
+    move_copy.wait()
+
+    def count_moved(i, _):
+        j = OWN - MOVED + i
+        for f in range(4):
+            a = x[f, j].astype(F32).reshape(256, 128)
+            v = jnp.where(heavy, a, moved[f, i].astype(F32).reshape(256, 128))
+            x[f, j] = v.astype(BF16).reshape(x.shape[2:])
+            add_up(f, j, v)
+        return 0
+
+    lax.fori_loop(0, MOVED, count_moved, 0)
+    for c in late:
+        c.start()
+    sums1 = [s_ref[f] for f in range(4)]
+    fill(sums1, mine1)
+    copies1 = share(mine1, got1, send1, recv1)
     norms(sums1, copies1, got1, gain1_ref, per_frame, p1)
-    halo_copy = to_right(xb_ref, halo, 0)
-    send(halo_copy)
-
-    def first_tiles(base, ra, rb):
-        def step(j, _):
+
+    def halo_copy(j):
+        return pltpu.make_async_remote_copy(
+            src_ref=x.at[2:4, j],
+            dst_ref=halo.at[:, j],
+            send_sem=hsend.at[j],
+            recv_sem=hrecv.at[j],
+            device_id={"tm": right},
+            device_id_type=MESH,
+        )
+
+    @pl.when(me < n - 1)
+    def _():
+        for j in range(OWN):
+            halo_copy(j).start()
+
+    def first_tiles(base, ready):
+        def frame(q, j):
+            if base == 2:
+                return x[q, j]
+            return halo[q, j] if q < 2 else x[q - 2, j]
+
+        def prep(j, z):
             for q in range(4):
-                x = (ra if q < 2 else rb)[q % 2, j].astype(F32).reshape(256, 128)
+                v = frame(q, j).astype(F32).reshape(256, 128)
                 mean = p1[base + q, 0, pl.ds(j, 1), :]
                 scale = p1[base + q, 1, pl.ds(j, 1), :]
-                h = silu((x - mean) * scale + shift1_ref[...])
+                h = silu((v - mean) * scale + shift1_ref[...])
                 left, right_ = shifted(h, 16)
                 k = (q % 2) * 384
-                buf[q // 2, 16:272, k : k + 128] = left.astype(BF16)
-                buf[q // 2, 16:272, k + 128 : k + 256] = h.astype(BF16)
-                buf[q // 2, 16:272, k + 256 : k + 384] = right_.astype(BF16)
+                buf[z, q // 2, 16:272, k : k + 128] = left.astype(BF16)
+                buf[z, q // 2, 16:272, k + 128 : k + 256] = h.astype(BF16)
+                buf[z, q // 2, 16:272, k + 256 : k + 384] = right_.astype(BF16)
+
+        def multiply(j, z):
             acc = jnp.zeros((256, 256), F32)
             for p in range(2):
                 for b in range(3):
                     acc = acc + jnp.dot(
-                        buf[p, b * 16 : b * 16 + 256, :], w2[p * 3 + b], preferred_element_type=F32
+                        buf[z, p, b * 16 : b * 16 + 256, :], w2[p * 3 + b], preferred_element_type=F32
                     )
             for e in range(2):
-                x = rb[e, j].astype(F32).reshape(256, 128)
-                sf[e] = (x + acc[:, e * 128 : e * 128 + 128]).astype(BF16).astype(F32)
+                v = frame(2 + e, j).astype(F32).reshape(256, 128)
+                sf[z, e] = (v + acc[:, e * 128 : e * 128 + 128]).astype(BF16).astype(F32)
             row = pl.multiple_of(j * 64, 64)
             col = lax.broadcasted_iota(jnp.int32, (128, 128), 0) % 8
             for e in range(2):
-                even = sf[e, pl.ds(0, 128, stride=2), :]
-                odd = sf[e, pl.ds(1, 128, stride=2), :]
+                even = sf[z, e, pl.ds(0, 128, stride=2), :]
+                odd = sf[z, e, pl.ds(1, 128, stride=2), :]
                 prev = jnp.where(col == 0, 0.0, pltpu.roll(odd, 1, axis=0))
                 for c, v in enumerate((prev, even, odd)):
                     v = v.reshape(8, 2, 8, 128)
@@ -298,15 +322,25 @@
                     k = e * 384 + c * 128
                     for b, u in enumerate((up, top, low)):
                         lhs[b, pl.ds(row, 64), k : k + 128] = u.reshape(64, 128).astype(BF16)
+
+        def step(i, _):
+            ready(2 * i + 1, True)
+            ready(2 * i + 2, i < OWN // 2 - 1)
+            prep(2 * i + 1, 1)
+            multiply(2 * i, 0)
+            prep(jnp.minimum(2 * i + 2, OWN - 1), 0)
+            multiply(2 * i + 1, 1)
             return 0
 
-        lax.fori_loop(0, OWN, step, 0)
+        ready(0, True)
+        prep(0, 0)
+        lax.fori_loop(0, OWN // 2, step, 0)
         out = jnp.zeros((512, 256), F32)
         for b in range(3):
             out = out + jnp.dot(lhs[b], wd[b], preferred_element_type=F32)
         return out
 
-    out = first_tiles(2, xa_ref, xb_ref)
+    out = first_tiles(2, lambda j, some: None)
     own1[...] = out[:, 0:128]
     next1[...] = out[:, 128:256]
     part_copy = to_right(next1, part1, 1)
@@ -314,11 +348,15 @@
 
     @pl.when(me == 0)
     def _():
-        halo[0] = xa_ref[0]
-        halo[1] = xa_ref[0]
-
-    landed(halo_copy)
-    out = first_tiles(0, halo, xa_ref)
+        halo[0] = x[0]
+        halo[1] = x[0]
+
+    def halo_ready(j, some):
+        @pl.when(jnp.logical_and(me > 0, some))
+        def _():
+            halo_copy(j).wait_recv()
+
+    out = first_tiles(0, halo_ready)
     level[1] = (own1[...] + out[:, 128:256]).astype(BF16)
     own1[...] = out[:, 0:128]
 
@@ -332,7 +370,12 @@
 
     landed(part_copy)
     level[0] = (own1[...] + part1[...]).astype(BF16)
-    sent(halo_copy)
+
+    @pl.when(me < n - 1)
+    def _():
+        for j in range(OWN):
+            halo_copy(j).wait_send()
+
     sent(part_copy)
 
     sums2 = []
@@ -355,10 +398,10 @@
         def step(t, _):
             rows = pl.ds(pl.multiple_of(t * 64, 64), 64)
             for q in range(2):
-                x = ref[q, rows, :].astype(F32)
+                v = ref[q, rows, :].astype(F32)
                 mean = p2[base + q, 0, pl.ds(t, 1), :]
                 scale = p2[base + q, 1, pl.ds(t, 1), :]
-                h = silu((x - mean) * scale + shift2_ref[...])
+                h = silu((v - mean) * scale + shift2_ref[...])
                 left, right_ = shifted(h, 8)
                 pad = jnp.zeros((8, 128), F32)
                 for c, v in enumerate((left, h, right_)):
@@ -374,12 +417,15 @@
     second_tiles(2, level)
     landed(lhalo_copy)
     second_tiles(0, lhalo)
+    late[0].wait()
     level2 = []
     for f in range(2):
         acc = jnp.dot(level[f], short_ref[...], preferred_element_type=F32)
         for a in range(3):
             acc = acc + jnp.dot(lhs2[f + a], conv2_ref[a], preferred_element_type=F32)
         level2.append(acc.astype(BF16))
+    late[1].wait()
+    late[2].wait()
     own = jnp.zeros((128, 256), F32)
     nxt = jnp.zeros((128, 256), F32)
     for i in range(9):
@@ -409,23 +455,26 @@
 
     landed(part2_copy)
     enc[...] = (own2[...] + part2[...]).astype(BF16)
-    swap = pltpu.make_async_remote_copy(
-        src_ref=enc,
-        dst_ref=renc,
-        send_sem=sems.at[8],
-        recv_sem=sems.at[9],
-        device_id={"tile": partner},
-        device_id_type=MESH,
-    )
-    swap.start()
-    out_ref[0] = enc[...]
+    enc_copy = swap(enc, renc, 4)
+    enc_copy.start()
+    info_copy.wait()
+    lane = lax.broadcasted_iota(jnp.int32, (1, 128), 1)
+    low = lane < (OWN - MOVED) * 16
+    my_ids = jnp.where(low | heavy, info_ref[0:1, :], rinfo[1:2, :])
+    its_ids = jnp.where(low | (rinfo[2:3, :] == 1), rinfo[0:1, :], info_ref[1:2, :])
+    row = lax.broadcasted_iota(jnp.int32, (128, 128), 0)
+    wanted = lax.axis_index("tile") * OWN + row // 16
+    cell = row % 16 == lax.broadcasted_iota(jnp.int32, (128, 128), 1) % 16
+    mine = jnp.where((wanted == my_ids) & cell, 1.0, 0.0).astype(BF16)
+    its = jnp.where((wanted == its_ids) & cell, 1.0, 0.0).astype(BF16)
+    kept = jnp.dot(mine, enc[...], preferred_element_type=F32)
     sent(lhalo_copy)
     sent(part2_copy)
-    swap.wait()
-    out_ref[1] = renc[...]
-
-
-def encode(xa, xb, sums, params, n):
+    enc_copy.wait()
+    out_ref[...] = (kept + jnp.dot(its, renc[...], preferred_element_type=F32)).astype(BF16)
+
+
+def encode(acts, info, params, n):
     (
         first_gain,
         first_shift,
@@ -437,16 +486,23 @@
         second_short,
         second_down,
     ) = params
-    cells = xa.shape[2:]
+    cells = acts.shape[2:]
     rows = OWN * 64
     vm = pltpu.VMEM
     line = lambda v: v.reshape(1, 128)
     return pl.pallas_call(
         functools.partial(main_kernel, n, float(cells[0] * cells[1] * (cells[2] // GROUPS))),
-        out_shape=jax.ShapeDtypeStruct((2, OWN * 16, 256), BF16),
-        in_specs=[VMEM] * 13,
+        out_shape=jax.ShapeDtypeStruct((OWN * 16, 256), BF16),
+        in_specs=[ANY] + [VMEM] * 7 + [ANY, VMEM, ANY, ANY],
         out_specs=VMEM,
         scratch_shapes=[
+            vm((4, OWN) + cells, BF16),
+            vm((4, MOVED) + cells, BF16),
+            vm((8, 128), jnp.int32),
+            vm((4, 2 * OWN, 128), F32),
+            vm((3, 1152, 256), BF16),
+            vm((27, 256, 256), BF16),
+            vm((9 * OWN * 16, rows), BF16),
             vm((2, 2 * OWN, 128), F32),
             vm((n, 2, 2 * OWN, 128), F32),
             vm((2, 2 * OWN, 128), F32),
@@ -454,10 +510,10 @@
             vm((6, 2, OWN, 128), F32),
             vm((4, 2, OWN, 128), F32),
             vm((2, OWN) + cells, BF16),
-            vm((2, 288, 768), BF16),
+            vm((2, 2, 288, 768), BF16),
             vm((6, 768, 256), BF16),
             vm((3, 768, 256), BF16),
-            vm((2, 256, 128), F32),
+            vm((2, 2, 256, 128), F32),
             vm((3, rows, 768), BF16),
             vm((rows, 128), F32),
             vm((rows, 128), F32),
@@ -474,14 +530,16 @@
             pltpu.SemaphoreType.DMA((n,)),
             pltpu.SemaphoreType.DMA((n,)),
             pltpu.SemaphoreType.DMA((n,)),
-            pltpu.SemaphoreType.DMA((10,)),
+            pltpu.SemaphoreType.DMA((14,)),
+            pltpu.SemaphoreType.DMA((OWN,)),
+            pltpu.SemaphoreType.DMA((OWN,)),
+            pltpu.SemaphoreType.DMA((4,)),
         ],
         name="encode",
         compiler_params=pltpu.CompilerParams(collective_id=0, has_side_effects=True, vmem_limit_bytes=LIMIT),
     )(
-        xa,
-        xb,
-        sums,
+        acts,
+        info,
         line(first_gain),
         line(first_shift),
         first_conv,
@@ -493,10 +551,6 @@
         second_down.reshape(27, 256, 256),
         jnp.asarray(pick_matrix(), BF16),
     )
-
-
-def swapped(value):
-    return lax.ppermute(value, "tile", [(0, 1), (1, 0)])
 
 
 def body(
@@ -514,23 +568,14 @@
     second_down,
 ):
     n = lax.axis_size("tm")
-    me = lax.axis_index("tile")
     cap = activations.shape[1]
-    recv = swapped(activations[:, OWN:cap])
-    info = jnp.concatenate([tile_ids, tile_counts])
-    other = swapped(info)
-    heavy = (tile_counts[0] == cap).astype(jnp.int32).reshape(1)
-
-    def encoded_ids(a, b):
-        slots = jnp.arange(cap)
-        ids_a = jnp.where(slots < a[cap], a[:cap], -1)
-        ids_b = jnp.where(slots < b[cap], b[:cap], -1)
-        kept = jnp.where(a[cap] == cap, ids_a[OWN - MOVED : OWN], ids_b[OWN:])
-        return jnp.concatenate([ids_a[: OWN - MOVED], kept])
-
-    ids = jnp.concatenate([encoded_ids(info, other), encoded_ids(other, info)])
-
-    xa, xb, sums = prep(activations, recv, heavy)
+    count = tile_counts[0]
+    ids = jnp.repeat(jnp.where(jnp.arange(cap) < count, tile_ids, -1), 16)
+    split = (OWN - MOVED) * 16
+    kept = ids[: OWN * 16]
+    mixed = jnp.concatenate([ids[:split], ids[OWN * 16 :]])
+    heavy = jnp.full((OWN * 16,), count == cap, jnp.int32)
+    info = jnp.stack([kept, mixed] + [heavy] * 6)
     params = (
         first_gain,
         first_shift,
@@ -542,9 +587,7 @@
         second_short,
         second_down,
     )
-    both = encode(xa, xb, sums, params, n).reshape(2 * OWN, 16 * 256)
-    select = (ids[None, :] == (me * OWN + jnp.arange(OWN))[:, None]).astype(BF16)
-    latents = jnp.dot(select, both, preferred_element_type=F32).astype(BF16)
+    latents = encode(activations, info, params, n)
     return latents.reshape(1, OWN, 4, 4, 256)
 
 

time: 78.5 us -> 66.1 us (0.84)
  Pallas kernels: 68.3 us -> 61.9 us
  local copies, waits for them, and re-layouts: 4.62 us -> 2.65 us
  other arithmetic: 2.19 us -> 0.74 us
    pallas_call x1 -> x0, Pallas kernels: 6.07 us -> none  [prep(): pl.pallas_call(prep_kernel, out_shape=(jax.ShapeDtypeStruct((2, OWN) + ce...]
    slice x2 -> x3, local copies, waits for them, and re-layouts: 1.99 us -> 0.24 us  [body(): mixed = jnp.concatenate([ids[:split], ids[OWN * 16:]])]
    unnamed x2 -> x0, local copies, waits for them, and re-layouts: 1 us -> none
    reshape x1 -> x0, local copies, waits for them, and re-layouts: 0.97 us -> none  [body(): both = encode(xa, xb, sums, params, n).reshape(2 * OWN, 16 * 256)]
    reshape x1, local copies, waits for them, and re-layouts: 0.66 us -> 1.49 us  [body(): return latents.reshape(1, OWN, 4, 4, 256)]
    concatenate x2 -> x0, other arithmetic: 0.81 us -> none  [the longest x1 0.73 us: body(): info = jnp.concatenate([tile_ids, tile_counts])]
  transfers between devices with their start and end apart: 2 -> 0, of which waited for: 1 -> 0; matrix products, arithmetic and copies ran while one was open for 4% -> 0% of each run, Pallas kernels for 0% -> 0%
where the time goes in v3:
time: 66.1 us; the launch traced here: 65.9 us
  Pallas kernels  61.9 us (94%)
  local copies, waits for them, and re-layouts  2.65 us (4%)
  other arithmetic  0.74 us (1%)
  between operations  0.68 us (1%)
    pallas_call x1, Pallas kernels, encode(): pl.pallas_call(functools.partial(main_kernel, n, float(cells[0] * cells[1...  61.9 us
    reshape x1, local copies, waits for them, and re-layouts, body(): return latents.reshape(1, OWN, 4, 4, 256)  1.49 us

profile of v3, /device:TPU:17, one launch (start us, length us, event | category | flops | bytes accessed | tf_op | source)
XLA Modules:
  0.0 65.9 jit_solution(16829809701437982180)
XLA Ops:
  0.7 0.7 %compare_select_fusion = s32[12]{0:T(128)S(1)} fusion(s32[12]{0:T(128)} %param.14, s32[]{:T(128)} %bitcast.10), kind=kLoop, calls=%fused_computation | loop fusion | flops 24 | bytes 100 | tf_op jit(solution)/shard_map/jit(_where)/select_n | solution.py:573
  1.3 0.1 fusion
  1.4 0.1 broadcast_in_dim.13
  1.5 0.1 slice.21
  1.6 0.1 broadcast_in_dim.14
  1.6 0.1 slice.23
  1.7 0.1 add_bitcast_fusion
  1.8 0.1 broadcast_in_dim.12
  1.9 0.1 stack.9
  1.9 0.6 stack.11.info_ref
  2.6 61.9 %encode.1 = bf16[128,256]{1,0:T(8,128)(2,1)} custom-call(bf16[4,12,16,16,128]{4,3,2,1,0:T(8,128)(2,1)} %act_ref.1, s32[8,128]{1,0:T(8,128)} %stack.11.info_ref, f32[1,128]{1,0:T(1,128)} %bitcast.15, f32[1,128]{1,0:T(1,128)} %bitcast.16, bf16[3,3,3,128,128]{4,3,2,1,0:T(8,128)(2,1)} %conv1_ref.1, bf16[3,3,3,128,128]{4,3,2,1,0:T(8,128)(2,1)} %down1_ref.1, ...), custom_call_target="tpu_custom_call" | custom-call | tf_op jit(solution)/shard_map/encode/pallas_call | solution.py:493
  64.5 1.5 %reshape.32 = bf16[1,8,4,4,256]{4,3,2,1,0:T(4,128)(2,1)} reshape(bf16[128,256]{1,0:T(8,128)(2,1)} %encode.1) | data formatting | bytes 131072 | tf_op jit(solution)/shard_map/reshape | solution.py:591
  (1 shorter events, 0.0 us)

commit v4 on v3

--- a/solution.py
+++ b/solution.py
@@ -264,8 +264,6 @@
     sums1 = [s_ref[f] for f in range(4)]
     fill(sums1, mine1)
     copies1 = share(mine1, got1, send1, recv1)
-    norms(sums1, copies1, got1, gain1_ref, per_frame, p1)
-
     def halo_copy(j):
         return pltpu.make_async_remote_copy(
             src_ref=x.at[2:4, j],
@@ -280,6 +278,8 @@
     def _():
         for j in range(OWN):
             halo_copy(j).start()
+
+    norms(sums1, copies1, got1, gain1_ref, per_frame, p1)
 
     def first_tiles(base, ready):
         def frame(q, j):

time: 66.1 us -> 64.4 us (0.974)
  Pallas kernels: 61.9 us -> 59.8 us
    pallas_call x1, Pallas kernels: 61.9 us -> 59.8 us  [encode(): pl.pallas_call(functools.partial(main_kernel, n, float(cells[0] * cells[1...]
where the time goes in v4:
time: 64.4 us; the launch traced here: 63.9 us
  Pallas kernels  59.8 us (93%)
  local copies, waits for them, and re-layouts  2.65 us (4%)
  other arithmetic  0.74 us (1%)
  between operations  0.68 us (1%)
    pallas_call x1, Pallas kernels, encode(): pl.pallas_call(functools.partial(main_kernel, n, float(cells[0] * cells[1...  59.8 us
    reshape x1, local copies, waits for them, and re-layouts, body(): return latents.reshape(1, OWN, 4, 4, 256)  1.49 us

profile of v4, /device:TPU:17, one launch (start us, length us, event | category | flops | bytes accessed | tf_op | source)
XLA Modules:
  0.0 63.9 jit_solution(4101496925271562498)
XLA Ops:
  0.7 0.7 %compare_select_fusion = s32[12]{0:T(128)S(1)} fusion(s32[12]{0:T(128)} %param.14, s32[]{:T(128)} %bitcast.10), kind=kLoop, calls=%fused_computation | loop fusion | flops 24 | bytes 100 | tf_op jit(solution)/shard_map/jit(_where)/select_n | solution.py:573
  1.3 0.1 fusion
  1.4 0.1 broadcast_in_dim.13
  1.5 0.1 slice.21
  1.6 0.1 broadcast_in_dim.14
  1.6 0.1 slice.23
  1.7 0.1 add_bitcast_fusion
  1.8 0.1 broadcast_in_dim.12
  1.9 0.1 stack.9
  1.9 0.6 stack.11.info_ref
  2.6 59.8 %encode.1 = bf16[128,256]{1,0:T(8,128)(2,1)} custom-call(bf16[4,12,16,16,128]{4,3,2,1,0:T(8,128)(2,1)} %act_ref.1, s32[8,128]{1,0:T(8,128)} %stack.11.info_ref, f32[1,128]{1,0:T(1,128)} %bitcast.15, f32[1,128]{1,0:T(1,128)} %bitcast.16, bf16[3,3,3,128,128]{4,3,2,1,0:T(8,128)(2,1)} %conv1_ref.1, bf16[3,3,3,128,128]{4,3,2,1,0:T(8,128)(2,1)} %down1_ref.1, ...), custom_call_target="tpu_custom_call" | custom-call | tf_op jit(solution)/shard_map/encode/pallas_call | solution.py:493
  62.4 1.5 %reshape.32 = bf16[1,8,4,4,256]{4,3,2,1,0:T(4,128)(2,1)} reshape(bf16[128,256]{1,0:T(8,128)(2,1)} %encode.1) | data formatting | bytes 131072 | tf_op jit(solution)/shard_map/reshape | solution.py:591
  (1 shorter events, 0.0 us)
